TPU v7x, 32 devices: a whole 2x2x4 slice. The times are simulated.
32 devices in a mesh: dp: 8 (over z, y), tensor: 4 (over x, core).
Axes of the slice: x: 2, y: 2, z: 4, core: 2. Of those that a mesh axis runs over, the one named last changes fastest.
Arguments:
- inputs: bfloat16 [8192, 1536], P('dp', 'tensor'), may hold values from -6 to 6
- segment_ids: int32 [8192], P('dp'), may hold values from 0 to 26, never falling along the last dimension, each value on 1 to 1000 neighbouring positions
- cotangent: bfloat16 [8192, 1536], P('dp', 'tensor'), may hold values from -6 to 6
- first_gain: bfloat16 [1536], replicated, may hold values from 0.5 to 1.5
- gate_weight: bfloat16 [1536, 2048], P(None, 'tensor'), may hold values from -0.15625 to 0.15625
- gate_bias: bfloat16 [2048], P('tensor'), may hold values from -3 to 3
- branch_weight: bfloat16 [1536, 2048], P(None, 'tensor'), may hold values from -0.15625 to 0.15625
- branch_bias: bfloat16 [2048], P('tensor'), may hold values from -3 to 3
- conv_weight: bfloat16 [4, 2048], P(None, 'tensor'), may hold values from -3 to 3
- conv_bias: bfloat16 [2048], P('tensor'), may hold values from -3 to 3
- rate_weight: bfloat16 [16, 128, 128], P('tensor'), may hold values from -0.5 to 0.5
- rate_bias: bfloat16 [2048], P('tensor'), may hold values from -3 to 3
- input_weight: bfloat16 [16, 128, 128], P('tensor'), may hold values from -0.5 to 0.5
- input_bias: bfloat16 [2048], P('tensor'), may hold values from -3 to 3
- decay_param: float32 [2048], P('tensor'), may hold values from 3 to 7
- out_weight: bfloat16 [2048, 1536], P('tensor'), may hold values from -0.25 to 0.25
- second_gain: bfloat16 [1536], replicated, may hold values from 0.5 to 1.5
- ffn_gate: bfloat16 [1536, 4608], P(None, 'tensor'), may hold values from -0.15625 to 0.15625
- ffn_up: bfloat16 [1536, 4608], P(None, 'tensor'), may hold values from -0.15625 to 0.15625
- ffn_down: bfloat16 [4608, 1536], P('tensor'), may hold values from -0.1875 to 0.1875
Outputs:
- output: bfloat16 [8192, 1536], P('dp', 'tensor')
- input_grad: float32 [8192, 1536], P('dp', 'tensor')
- first_gain_grad: float32 [1536], replicated
- gate_weight_grad: float32 [1536, 2048], P(None, 'tensor')
- gate_bias_grad: float32 [2048], P('tensor')
- branch_weight_grad: float32 [1536, 2048], P(None, 'tensor')
- branch_bias_grad: float32 [2048], P('tensor')
- conv_weight_grad: float32 [4, 2048], P(None, 'tensor')
- conv_bias_grad: float32 [2048], P('tensor')
- rate_weight_grad: float32 [16, 128, 128], P('tensor')
- rate_bias_grad: float32 [2048], P('tensor')
- input_weight_grad: float32 [16, 128, 128], P('tensor')
- input_bias_grad: float32 [2048], P('tensor')
- decay_grad: float32 [2048], P('tensor')
- out_weight_grad: float32 [2048, 1536], P('tensor')
- second_gain_grad: float32 [1536], replicated
- ffn_gate_grad: float32 [1536, 4608], P(None, 'tensor')
- ffn_up_grad: float32 [1536, 4608], P(None, 'tensor')
- ffn_down_grad: float32 [4608, 1536], P('tensor')
Inputs may be any that keep to these rules, and one draw needn't show every extreme that they name: `segment_ids`: segment numbers never fall along the tokens; each document has 1 to 1000 consecutive tokens, one exactly 1000.
All inputs are finite; a program needn't handle non-finite values.
Results may differ from a plain program's by a relative error of at most 0.013.
Values may be sent and summed in bfloat16 or wider, within the bound.
A program may use at most 256 MiB of HBM per device.

v0:
```python
import jax
import jax.numpy as jnp
from jax import lax
from jax.sharding import PartitionSpec as P

SEQ = 1024


EPSILON = 1e-06
FLOOR = 0.05


def rms_scale(values, gain):
    return values * lax.rsqrt(jnp.mean(values * values, axis=-1, keepdims=True) + EPSILON) * gain


def seq_masks(segments, length):
    count = segments.shape[0]
    place = jnp.arange(count, dtype=jnp.int32) % length
    previous = jnp.concatenate([segments[:1], segments[:-1]])
    reset = (place == 0) | (segments != previous)
    return (place, reset)


def conv_apply(values, weights, shift_bias, segments, place):
    total = shift_bias + weights[0] * values
    for offset in range(1, weights.shape[0]):
        moved = jnp.concatenate(
            [jnp.zeros((offset, values.shape[1]), values.dtype), values[:-offset]]
        )
        earlier = jnp.concatenate([jnp.full((offset,), -1, jnp.int32), segments[:-offset]])
        usable = ((place >= offset) & (segments == earlier)).astype(values.dtype)
        total = total + weights[offset] * moved * usable[:, None]
    return total


def gates_to_step(rate_pre, input_pre, conv_out, decay, reset):
    rate = jax.nn.sigmoid(rate_pre)
    opened = jax.nn.sigmoid(input_pre)
    decayed = jnp.exp(-8.0 * rate * jax.nn.softplus(-decay))
    keep = jnp.where(reset[:, None], jnp.zeros_like(decayed), decayed)
    scale = jnp.where(
        reset[:, None],
        jnp.ones_like(decayed),
        jnp.sqrt(jnp.maximum(1.0 - decayed * decayed, FLOOR)),
    )
    return (keep, scale * opened * conv_out)


def combine(earlier, later):
    return (earlier[0] * later[0], later[0] * earlier[1] + later[1])


def block_mix(values, weight):
    rows = values.shape[0]
    split = values.reshape(rows, weight.shape[0], -1)
    return jnp.einsum("thi,hij->thj", split, weight, preferred_element_type=jnp.float32).reshape(
        rows, -1
    )


def block_back(grads, weight):
    rows = grads.shape[0]
    split = grads.reshape(rows, weight.shape[0], -1)
    return jnp.einsum("thj,hij->thi", split, weight, preferred_element_type=jnp.float32).reshape(
        rows, -1
    )


def block_grad(values, grads, heads):
    rows = values.shape[0]
    left = values.reshape(rows, heads, -1)
    right = grads.reshape(rows, heads, -1)
    return jnp.einsum("thi,thj->hij", left, right, preferred_element_type=jnp.float32)


def column_sum(values):
    return jnp.sum(values.astype(jnp.float32), axis=0)


def body(
    inputs,
    segment_ids,
    cotangent,
    first_gain,
    gate_weight,
    gate_bias,
    branch_weight,
    branch_bias,
    conv_weight,
    conv_bias,
    rate_weight,
    rate_bias,
    input_weight,
    input_bias,
    decay_param,
    out_weight,
    second_gain,
    ffn_gate,
    ffn_up,
    ffn_down,
):
    share = inputs.shape[1]
    heads = rate_weight.shape[0]
    offset = lax.axis_index("tensor") * share
    place, reset = seq_masks(segment_ids, SEQ)
    whole_in = lax.all_gather(inputs, "tensor", axis=1, tiled=True).astype(jnp.float32)
    normed_one, first_pull = jax.vjp(rms_scale, whole_in, first_gain.astype(jnp.float32))
    normed_low = normed_one.astype(jnp.bfloat16)
    gate_pre = jnp.dot(
        normed_low, gate_weight, preferred_element_type=jnp.float32
    ) + gate_bias.astype(jnp.float32)
    branch_pre = jnp.dot(
        normed_low, branch_weight, preferred_element_type=jnp.float32
    ) + branch_bias.astype(jnp.float32)

    def conv_local(values, weights, shift_bias):
        return conv_apply(values, weights, shift_bias, segment_ids, place)

    conv_out, conv_pull = jax.vjp(
        conv_local, branch_pre, conv_weight.astype(jnp.float32), conv_bias.astype(jnp.float32)
    )
    conv_low = conv_out.astype(jnp.bfloat16)
    rate_pre = block_mix(conv_low, rate_weight) + rate_bias.astype(jnp.float32)
    input_pre = block_mix(conv_low, input_weight) + input_bias.astype(jnp.float32)

    def step_local(rate_in, input_in, driven, decay):
        return gates_to_step(rate_in, input_in, driven, decay, reset)

    (keep, drive), step_pull = jax.vjp(step_local, rate_pre, input_pre, conv_out, decay_param)
    state = lax.associative_scan(combine, (keep, drive))[1]
    gate_act, gelu_pull = jax.vjp(jax.nn.gelu, gate_pre)
    mixed_low = (gate_act * state).astype(jnp.bfloat16)
    partial_value = jnp.dot(mixed_low, out_weight, preferred_element_type=jnp.float32)
    resid = whole_in + lax.psum(partial_value, "tensor")
    resid_mine = lax.dynamic_slice_in_dim(resid, offset, share, 1)
    normed_two, second_pull = jax.vjp(rms_scale, resid, second_gain.astype(jnp.float32))
    two_low = normed_two.astype(jnp.bfloat16)
    hidden_gate = jnp.dot(two_low, ffn_gate, preferred_element_type=jnp.float32)
    hidden_up = jnp.dot(two_low, ffn_up, preferred_element_type=jnp.float32)
    hidden_act, hidden_pull = jax.vjp(jax.nn.gelu, hidden_gate)
    hidden_low = (hidden_act * hidden_up).astype(jnp.bfloat16)
    ffn_part = jnp.dot(hidden_low, ffn_down, preferred_element_type=jnp.float32)
    output = (
        resid_mine
        + lax.psum_scatter(
            ffn_part.astype(jnp.bfloat16), "tensor", scatter_dimension=1, tiled=True
        ).astype(jnp.float32)
    ).astype(jnp.bfloat16)
    whole_cot = lax.all_gather(cotangent, "tensor", axis=1, tiled=True)
    d_hidden = jnp.einsum("td,fd->tf", whole_cot, ffn_down, preferred_element_type=jnp.float32)
    ffn_down_grad = jnp.einsum(
        "tf,td->fd", hidden_low, whole_cot, preferred_element_type=jnp.float32
    )
    d_hgate = hidden_pull(d_hidden * hidden_up)[0].astype(jnp.bfloat16)
    d_hup = (d_hidden * hidden_act).astype(jnp.bfloat16)
    ffn_gate_grad = jnp.einsum("td,tf->df", two_low, d_hgate, preferred_element_type=jnp.float32)
    ffn_up_grad = jnp.einsum("td,tf->df", two_low, d_hup, preferred_element_type=jnp.float32)
    d_two_part = jnp.einsum(
        "tf,df->td", d_hgate, ffn_gate, preferred_element_type=jnp.float32
    ) + jnp.einsum("tf,df->td", d_hup, ffn_up, preferred_element_type=jnp.float32)
    d_two = lax.psum(d_two_part, "tensor")
    d_resid_norm, second_gain_grad = second_pull(d_two)
    d_resid = whole_cot.astype(jnp.float32) + d_resid_norm
    d_resid_low = d_resid.astype(jnp.bfloat16)
    out_weight_grad = jnp.einsum(
        "tr,td->rd", mixed_low, d_resid_low, preferred_element_type=jnp.float32
    )
    d_mixed = jnp.einsum("td,rd->tr", d_resid_low, out_weight, preferred_element_type=jnp.float32)
    d_gate_low = gelu_pull(d_mixed * state)[0].astype(jnp.bfloat16)
    d_state = d_mixed * gate_act
    channels = keep.shape[1]
    keep_next = jnp.concatenate([keep[1:], jnp.zeros((1, channels), jnp.float32)])
    adjoint = lax.associative_scan(combine, (keep_next, d_state), reverse=True)[1]
    state_prev = jnp.concatenate([jnp.zeros((1, channels), jnp.float32), state[:-1]])
    d_rate, d_input, d_conv_direct, decay_grad = step_pull((adjoint * state_prev, adjoint))
    d_rate_low = d_rate.astype(jnp.bfloat16)
    d_input_low = d_input.astype(jnp.bfloat16)
    rate_weight_grad = block_grad(conv_low, d_rate_low, heads)
    input_weight_grad = block_grad(conv_low, d_input_low, heads)
    rate_bias_grad = column_sum(d_rate_low)
    input_bias_grad = column_sum(d_input_low)
    d_conv = (
        d_conv_direct + block_back(d_rate_low, rate_weight) + block_back(d_input_low, input_weight)
    )
    d_branch, conv_weight_grad, conv_bias_grad = conv_pull(d_conv)
    d_branch_low = d_branch.astype(jnp.bfloat16)
    gate_weight_grad = jnp.einsum(
        "td,tr->dr", normed_low, d_gate_low, preferred_element_type=jnp.float32
    )
    branch_weight_grad = jnp.einsum(
        "td,tr->dr", normed_low, d_branch_low, preferred_element_type=jnp.float32
    )
    gate_bias_grad = column_sum(d_gate_low)
    branch_bias_grad = column_sum(d_branch_low)
    d_first_part = jnp.einsum(
        "tr,dr->td", d_gate_low, gate_weight, preferred_element_type=jnp.float32
    ) + jnp.einsum("tr,dr->td", d_branch_low, branch_weight, preferred_element_type=jnp.float32)
    d_first = lax.psum(d_first_part.astype(jnp.bfloat16), "tensor").astype(jnp.float32)
    d_in_norm, first_gain_grad = first_pull(d_first)
    input_grad = lax.dynamic_slice_in_dim(d_resid + d_in_norm, offset, share, 1)
    pieces = (
        lax.psum_scatter(first_gain_grad, "dp", scatter_dimension=0, tiled=True),
        lax.psum_scatter(gate_weight_grad, "dp", scatter_dimension=0, tiled=True),
        lax.psum_scatter(gate_bias_grad, "dp", scatter_dimension=0, tiled=True),
        lax.psum_scatter(branch_weight_grad, "dp", scatter_dimension=0, tiled=True),
        lax.psum_scatter(branch_bias_grad, "dp", scatter_dimension=0, tiled=True),
        lax.psum_scatter(conv_weight_grad, "dp", scatter_dimension=1, tiled=True),
        lax.psum_scatter(conv_bias_grad, "dp", scatter_dimension=0, tiled=True),
        lax.psum_scatter(rate_weight_grad, "dp", scatter_dimension=1, tiled=True),
        lax.psum_scatter(rate_bias_grad, "dp", scatter_dimension=0, tiled=True),
        lax.psum_scatter(input_weight_grad, "dp", scatter_dimension=1, tiled=True),
        lax.psum_scatter(input_bias_grad, "dp", scatter_dimension=0, tiled=True),
        lax.psum_scatter(decay_grad, "dp", scatter_dimension=0, tiled=True),
        lax.psum_scatter(out_weight_grad, "dp", scatter_dimension=0, tiled=True),
        lax.psum_scatter(second_gain_grad, "dp", scatter_dimension=0, tiled=True),
        lax.psum_scatter(ffn_gate_grad, "dp", scatter_dimension=0, tiled=True),
        lax.psum_scatter(ffn_up_grad, "dp", scatter_dimension=0, tiled=True),
        lax.psum_scatter(ffn_down_grad, "dp", scatter_dimension=1, tiled=True),
    )
    done = (
        lax.all_gather(pieces[0].astype(jnp.bfloat16), "dp", axis=0, tiled=True).astype(
            jnp.float32
        ),
        lax.all_gather(pieces[1].astype(jnp.bfloat16), "dp", axis=0, tiled=True).astype(
            jnp.float32
        ),
        lax.all_gather(pieces[2].astype(jnp.bfloat16), "dp", axis=0, tiled=True).astype(
            jnp.float32
        ),
        lax.all_gather(pieces[3].astype(jnp.bfloat16), "dp", axis=0, tiled=True).astype(
            jnp.float32
        ),
        lax.all_gather(pieces[4].astype(jnp.bfloat16), "dp", axis=0, tiled=True).astype(
            jnp.float32
        ),
        lax.all_gather(pieces[5].astype(jnp.bfloat16), "dp", axis=1, tiled=True).astype(
            jnp.float32
        ),
        lax.all_gather(pieces[6].astype(jnp.bfloat16), "dp", axis=0, tiled=True).astype(
            jnp.float32
        ),
        lax.all_gather(pieces[7].astype(jnp.bfloat16), "dp", axis=1, tiled=True).astype(
            jnp.float32
        ),
        lax.all_gather(pieces[8].astype(jnp.bfloat16), "dp", axis=0, tiled=True).astype(
            jnp.float32
        ),
        lax.all_gather(pieces[9].astype(jnp.bfloat16), "dp", axis=1, tiled=True).astype(
            jnp.float32
        ),
        lax.all_gather(pieces[10].astype(jnp.bfloat16), "dp", axis=0, tiled=True).astype(
            jnp.float32
        ),
        lax.all_gather(pieces[11].astype(jnp.bfloat16), "dp", axis=0, tiled=True).astype(
            jnp.float32
        ),
        lax.all_gather(pieces[12].astype(jnp.bfloat16), "dp", axis=0, tiled=True).astype(
            jnp.float32
        ),
        lax.all_gather(pieces[13].astype(jnp.bfloat16), "dp", axis=0, tiled=True).astype(
            jnp.float32
        ),
        lax.all_gather(pieces[14].astype(jnp.bfloat16), "dp", axis=0, tiled=True).astype(
            jnp.float32
        ),
        lax.all_gather(pieces[15].astype(jnp.bfloat16), "dp", axis=0, tiled=True).astype(
            jnp.float32
        ),
        lax.all_gather(pieces[16].astype(jnp.bfloat16), "dp", axis=1, tiled=True).astype(
            jnp.float32
        ),
    )
    return (
        output,
        input_grad,
        done[0],
        done[1],
        done[2],
        done[3],
        done[4],
        done[5],
        done[6],
        done[7],
        done[8],
        done[9],
        done[10],
        done[11],
        done[12],
        done[13],
        done[14],
        done[15],
        done[16],
    )


def solution(mesh):
    in_specs = (
        P("dp", "tensor"),
        P("dp"),
        P("dp", "tensor"),
        P(),
        P(None, "tensor"),
        P("tensor"),
        P(None, "tensor"),
        P("tensor"),
        P(None, "tensor"),
        P("tensor"),
        P("tensor", None, None),
        P("tensor"),
        P("tensor", None, None),
        P("tensor"),
        P("tensor"),
        P("tensor", None),
        P(),
        P(None, "tensor"),
        P(None, "tensor"),
        P("tensor", None),
    )
    out_specs = (
        P("dp", "tensor"),
        P("dp", "tensor"),
        P(),
        P(None, "tensor"),
        P("tensor"),
        P(None, "tensor"),
        P("tensor"),
        P(None, "tensor"),
        P("tensor"),
        P("tensor", None, None),
        P("tensor"),
        P("tensor", None, None),
        P("tensor"),
        P("tensor"),
        P("tensor", None),
        P(),
        P(None, "tensor"),
        P(None, "tensor"),
        P("tensor", None),
    )
    return jax.shard_map(body, mesh=mesh, in_specs=in_specs, out_specs=out_specs, check_vma=False)
```

profile of v0, /device:TPU:0, one launch (start us, length us, event | category | flops | bytes accessed | tf_op | source)
XLA Modules:
  0.0 2208.3 jit_solution(8797544625298831027)
XLA Ops:
  21.3 19.5 all-gather.10.cloned.1.call-done
  319.2 118.9 %all-reduce.76.cloned.1.call-done = f32[1024,1536]{1,0:T(8,128)} async-done(((f32[1024,1536]{1,0:T(8,128)}), f32[1024,1536]{1,0:T(8,128)}) %all-reduce.76.cloned.1.call-update) | async-done | bytes 6291472 | tf_op jit(solution)/shard_map/psum | solution.py:135
  458.7 9.7 all-gather.12.cloned.1.call-done
  468.4 12.3 multiply_convert_fusion.2
  531.4 9.1 slice.610
  544.6 66.4 %all-reduce.78.cloned.1.call-done = f32[1024,1536]{1,0:T(8,128)} async-done(((f32[1024,1536]{1,0:T(8,128)}), f32[1024,1536]{1,0:T(8,128)}) %all-reduce.78.cloned.1.call-update) | async-done | bytes 6291472 | tf_op jit(solution)/shard_map/psum | solution.py:162
  640.5 8.9 slice.614
  649.5 8.9 slice.616
  848.8 9.1 slice.688
  874.2 16.6 rev.2
  942.7 9.9 fusion.123
  952.7 10.0 fusion.124
  963.0 9.9 fusion.125
  1007.9 73.1 %reduce-scatter.23.cloned.1.call-done = f32[64,1536]{1,0:T(8,128)} async-done(((f32[512,1536]{1,0:T(8,128)}), f32[64,1536]{1,0:T(8,128)}) %reduce-scatter.23.cloned.1.call-update) | async-done | bytes 393232 | tf_op jit(solution)/shard_map/reduce_scatter | solution.py:215
  1082.8 75.1 %reduce-scatter.15.cloned.1.call-done = f32[192,512]{1,0:T(8,128)} async-done(((f32[1536,512]{1,0:T(8,128)}), f32[192,512]{1,0:T(8,128)}) %reduce-scatter.15.cloned.1.call-update) | async-done | bytes 393232 | tf_op jit(solution)/shard_map/reduce_scatter | solution.py:204
  1159.7 130.8 %reduce-scatter.25.cloned.1.call-done = f32[192,1152]{1,0:T(8,128)} async-done(((f32[1536,1152]{1,0:T(8,128)}), f32[192,1152]{1,0:T(8,128)}) %reduce-scatter.25.cloned.1.call-update) | async-done | bytes 884752 | tf_op jit(solution)/shard_map/reduce_scatter | solution.py:217
  1292.5 130.5 %reduce-scatter.27.cloned.1.call-done = f32[192,1152]{1,0:T(8,128)} async-done(((f32[1536,1152]{1,0:T(8,128)}), f32[192,1152]{1,0:T(8,128)}) %reduce-scatter.27.cloned.1.call-update) | async-done | bytes 884752 | tf_op jit(solution)/shard_map/reduce_scatter | solution.py:218
  1425.1 130.3 %reduce-scatter.29.cloned.1.call-done = f32[1152,192]{0,1:T(8,128)} async-done(((f32[1152,1536]{0,1:T(8,128)}), f32[1152,192]{0,1:T(8,128)}) %reduce-scatter.29.cloned.1.call-update) | async-done | bytes 884752 | tf_op jit(solution)/shard_map/reduce_scatter | solution.py:219
  1566.1 54.5 %reduce-scatter.33.cloned.1.call-done = f32[64,4]{1,0:T(8,128)} async-done(((f32[512,4]{1,0:T(8,128)}), f32[64,4]{1,0:T(8,128)}) %reduce-scatter.33.cloned.1.call-update) | async-done | bytes 1040
  1621.4 18.6 all-gather
  1640.7 45.2 %reduce-scatter.19.cloned.1.call-done = f32[4,16,128]{2,1,0:T(8,128)} async-done(((f32[4,128,128]{2,1,0:T(8,128)}), f32[4,16,128]{2,1,0:T(8,128)}) %reduce-scatter.19.cloned.1.call-update) | async-done | bytes 32784 | tf_op jit(solution)/shard_map/reduce_scatter | solution.py:210
  1686.7 30.5 %all_gather.66 = bf16[4,128,128]{2,1,0:T(8,128)(2,1)S(1)} all-gather(bf16[4,16,128]{2,1,0:T(8,128)(2,1)S(1)} %convert_element_type.250), channel_id=1, replica_groups=mesh['dp'=8,'tensor'=4] {'dp'}, dimensions={1}, use_global_device_ids=true | all-gather | bytes 147456 | tf_op jit(solution)/shard_map/all_gather | solution.py:243
  1717.9 33.5 %reduce-scatter.21.cloned.1.call-done = f32[4,16,128]{2,1,0:T(8,128)} async-done(((f32[4,128,128]{2,1,0:T(8,128)}), f32[4,16,128]{2,1,0:T(8,128)}) %reduce-scatter.21.cloned.1.call-update) | async-done | bytes 32784 | tf_op jit(solution)/shard_map/reduce_scatter | solution.py:212
  1752.2 30.8 %all_gather.68 = bf16[4,128,128]{2,1,0:T(8,128)(2,1)S(1)} all-gather(bf16[4,16,128]{2,1,0:T(8,128)(2,1)S(1)} %convert_element_type.255), channel_id=1, replica_groups=mesh['dp'=8,'tensor'=4] {'dp'}, dimensions={1}, use_global_device_ids=true | all-gather | bytes 147456 | tf_op jit(solution)/shard_map/all_gather | solution.py:249
  1783.7 38.0 %all-reduce.80.cloned.1.call-done = bf16[1024,1536]{1,0:T(8,128)(2,1)} async-done(((bf16[1024,1536]{1,0:T(8,128)(2,1)}), bf16[1024,1536]{1,0:T(8,128)(2,1)}) %all-reduce.80.cloned.1.call-update) | async-done | bytes 3145744 | tf_op jit(solution)/shard_map/psum | solution.py:199
  1828.6 38.4 %all-reduce.70 = (bf16[1536]{0:T(1024)(128)(2,1)}, bf16[512]{0:T(512)(128)(2,1)}, bf16[512]{0:T(512)(128)(2,1)}, bf16[512]{0:T(512)(128)(2,1)}, bf16[512]{0:T(51...) all-reduce(f32[1536]{0:T(1024)} %get-tuple-element.116, ...), channel_id=3, replica_groups=mesh['dp'=8,'tensor'=4] {'dp'}, use_global_device_ids=true, to_apply=%region_9.10.clone | all-reduce | flops 6144 | bytes 36864
  1886.2 34.5 %all-reduce.71 = (bf16[1536]{0:T(1024)(128)(2,1)}, bf16[512]{0:T(512)(128)(2,1)}, bf16[512]{0:T(512)(128)(2,1)}, bf16[512]{0:T(512)(128)(2,1)}, bf16[512]{0:T(51...) all-reduce(bf16[1536]{0:T(1024)(128)(2,1)S(1)} %dynamic-update-slic, ...), channel_id=1, replica_groups=mesh['dp'=8,'tensor'=4] {'dp'}, use_global_device_ids=true, to_apply=%add.54 | all-reduce | flops 6144 | bytes 24576
  1944.0 10.5 all-gather.18.cloned.1.call-done
  1958.0 41.1 %all-gather.14.cloned.1.call-done = bf16[1536,512]{1,0:T(8,128)(2,1)} async-done(((bf16[192,512]{1,0:T(8,128)(2,1)}), bf16[1536,512]{1,0:T(8,128)(2,1)}) %all-gather.14.cloned.1.call-update) | async-done | bytes 1572880 | tf_op jit(solution)/shard_map/all_gather | solution.py:225
  2002.6 61.7 %all-gather.20.cloned.1.call-done = bf16[1536,1152]{1,0:T(8,128)(2,1)} async-done(((bf16[192,1152]{1,0:T(8,128)(2,1)}), bf16[1536,1152]{1,0:T(8,128)(2,1)}) %all-gather.20.cloned.1.call-update) | async-done | bytes 3538960 | tf_op jit(solution)/shard_map/all_gather | solution.py:264
  2069.7 60.0 %all-gather.22.cloned.1.call-done = bf16[1536,1152]{1,0:T(8,128)(2,1)} async-done(((bf16[192,1152]{1,0:T(8,128)(2,1)}), bf16[1536,1152]{1,0:T(8,128)(2,1)}) %all-gather.22.cloned.1.call-update) | async-done | bytes 3538960 | tf_op jit(solution)/shard_map/all_gather | solution.py:267
  2135.1 60.1 %all-gather.24.cloned.1.call-done = bf16[1152,1536]{0,1:T(8,128)(2,1)} async-done(((bf16[1152,192]{0,1:T(8,128)(2,1)}), bf16[1152,1536]{0,1:T(8,128)(2,1)}) %all-gather.24.cloned.1.call-update) | async-done | bytes 3538960 | tf_op jit(solution)/shard_map/all_gather | solution.py:270
  (557 shorter events, 783.7 us)
Async XLA Ops:
  7.2 461.2 %copy-start = (bf16[1152,1536]{1,0:T(8,128)(2,1)S(1)}, bf16[1152,1536]{1,0:T(8,128)(2,1)}, u32[]{:S(2)}) copy-start(bf16[1152,1536]{1,0:T(8,128)(2,1)} %param.39) | copy-start | bytes 10616836
  7.2 33.6 %all-gather.10.cloned.1.call-start = ((), (), s32[]{:S(2)}) async-start(), calls=%async_computation.10 | async-start | bytes 3932160 | tf_op jit(solution)/shard_map/all_gather | solution.py:107
  7.9 430.2 %all-reduce.76.cloned.1.call-start = ((), (), s32[]{:S(2)}) async-start(), calls=%async_computation.11 | async-start | bytes 12582912 | tf_op jit(solution)/shard_map/psum | solution.py:135
  13.9 51.0 %copy-start.15 = (f32[512]{0:T(512)}, f32[512]{0:T(512)S(1)}, u32[]{:S(2)}) copy-start(f32[512]{0:T(512)S(1)} %convert_element_type.215) | copy-start | bytes 6148
  21.3 26.2 %copy-start.17 = (f32[1024]{0:T(1024)}, f32[1024]{0:T(1024)S(1)}, u32[]{:S(2)}) copy-start(f32[1024]{0:T(1024)S(1)} %get-tuple-element.209) | copy-start | bytes 12292
  21.3 26.2 %copy-start.19 = (f32[1024]{0:T(1024)}, f32[1024]{0:T(1024)S(1)}, u32[]{:S(2)}) copy-start(f32[1024]{0:T(1024)S(1)} %get-tuple-element.214) | copy-start | bytes 12292
  21.3 26.2 %copy-start.21 = (f32[1024]{0:T(1024)}, f32[1024]{0:T(1024)S(1)}, u32[]{:S(2)}) copy-start(f32[1024]{0:T(1024)S(1)} %get-tuple-element.215) | copy-start | bytes 12292
  234.5 18.4 copy-start.55
  318.4 150.0 %all-gather.12.cloned.1.call-start = ((), (), s32[]{:S(2)}) async-start(), calls=%async_computation.12 | async-start | bytes 3932160 | tf_op jit(solution)/shard_map/all_gather | solution.py:150
  319.1 291.9 %all-reduce.78.cloned.1.call-start = ((), (), s32[]{:S(2)}) async-start(), calls=%async_computation.13 | async-start | bytes 12582912 | tf_op jit(solution)/shard_map/psum | solution.py:162
  491.2 514.9 %reduce-scatter.17.cloned.1.call-start = ((), (), s32[]{:S(2)}) async-start(), calls=%async_computation.17 | async-start | bytes 3538944 | tf_op jit(solution)/shard_map/reduce_scatter | solution.py:206
  790.8 18.4 copy-start.56
  929.7 151.3 %reduce-scatter.23.cloned.1.call-start = ((), (), s32[]{:S(2)}) async-start(), calls=%async_computation.21 | async-start | bytes 3538944 | tf_op jit(solution)/shard_map/reduce_scatter | solution.py:215
  936.8 221.1 %reduce-scatter.15.cloned.1.call-start = ((), (), s32[]{:S(2)}) async-start(), calls=%async_computation.15 | async-start | bytes 3538944 | tf_op jit(solution)/shard_map/reduce_scatter | solution.py:204
  942.7 347.8 %reduce-scatter.25.cloned.1.call-start = ((), (), s32[]{:S(2)}) async-start(), calls=%async_computation.23 | async-start | bytes 7962624 | tf_op jit(solution)/shard_map/reduce_scatter | solution.py:217
  952.7 470.3 %reduce-scatter.27.cloned.1.call-start = ((), (), s32[]{:S(2)}) async-start(), calls=%async_computation.25 | async-start | bytes 7962624 | tf_op jit(solution)/shard_map/reduce_scatter | solution.py:218
  962.8 592.7 %reduce-scatter.29.cloned.1.call-start = ((), (), s32[]{:S(2)}) async-start(), calls=%async_computation.27 | async-start | bytes 7962624 | tf_op jit(solution)/shard_map/reduce_scatter | solution.py:219
  972.9 647.7 %reduce-scatter.33.cloned.1.call-start = ((), (), s32[]{:S(2)}) async-start(), calls=%async_computation.30 | async-start | bytes 294912
  975.2 710.8 %reduce-scatter.19.cloned.1.call-start = ((), (), s32[]{:S(2)}) async-start(), calls=%async_computation.19 | async-start | bytes 294912 | tf_op jit(solution)/shard_map/reduce_scatter | solution.py:210
  977.9 773.5 %reduce-scatter.21.cloned.1.call-start = ((), (), s32[]{:S(2)}) async-start(), calls=%async_computation.20 | async-start | bytes 294912 | tf_op jit(solution)/shard_map/reduce_scatter | solution.py:212
  986.8 834.9 %all-reduce.80.cloned.1.call-start = ((), (), s32[]{:S(2)}) async-start(), calls=%async_computation.14 | async-start | bytes 6291456 | tf_op jit(solution)/shard_map/psum | solution.py:199
  994.0 941.3 %reduce-scatter.31.cloned.1.call-start = ((), (), s32[]{:S(2)}) async-start(), calls=%async_computation.29 | async-start | bytes 3932160
  1006.1 934.4 %all-gather.16.cloned.1.call-start = ((), (), s32[]{:S(2)}) async-start(), calls=%async_computation.18 | async-start | bytes 1769472 | tf_op jit(solution)/shard_map/all_gather | solution.py:231
  1007.9 946.6 %all-gather.18.cloned.1.call-start = ((), (), s32[]{:S(2)}) async-start(), calls=%async_computation.22 | async-start | bytes 1769472 | tf_op jit(solution)/shard_map/all_gather | solution.py:258
  1082.7 916.4 %all-gather.14.cloned.1.call-start = ((), (), s32[]{:S(2)}) async-start(), calls=%async_computation.16 | async-start | bytes 1769472 | tf_op jit(solution)/shard_map/all_gather | solution.py:225
  1159.6 904.7 %all-gather.20.cloned.1.call-start = ((), (), s32[]{:S(2)}) async-start(), calls=%async_computation.24 | async-start | bytes 3981312 | tf_op jit(solution)/shard_map/all_gather | solution.py:264
  1292.4 265.0 %copy-start.63 = (u32[32]{0:T(128)S(1)}, u32[32]{0:T(128)}, u32[]{:S(2)}) copy-start(u32[32]{0:T(128)} %constant.193) | copy-start | bytes 388
  1292.5 837.2 %all-gather.22.cloned.1.call-start = ((), (), s32[]{:S(2)}) async-start(), calls=%async_computation.26 | async-start | bytes 3981312 | tf_op jit(solution)/shard_map/all_gather | solution.py:267
  1425.0 770.2 %all-gather.24.cloned.1.call-start = ((), (), s32[]{:S(2)}) async-start(), calls=%async_computation.28 | async-start | bytes 3981312 | tf_op jit(solution)/shard_map/all_gather | solution.py:270
  1783.7 44.9 %copy-start.29 = (f32[1536]{0:T(1024)S(1)}, f32[1536]{0:T(1024)}, u32[]{:S(2)}) copy-start(f32[1536]{0:T(1024)} %get-tuple-element.114) | copy-start | bytes 18436
  1783.7 147.1 %copy-start.28 = (f32[1024]{0:T(1024)S(1)}, f32[1024]{0:T(1024)}, u32[]{:S(2)}) copy-start(f32[1024]{0:T(1024)} %copy-done.27) | copy-start | bytes 12292
  1783.7 147.8 %copy-start.26 = (f32[1024]{0:T(1024)S(1)}, f32[1024]{0:T(1024)}, u32[]{:S(2)}) copy-start(f32[1024]{0:T(1024)} %copy-done.23) | copy-start | bytes 12292
  (69 other events, 392.1 us)
Sparse Core Ops, SparseCore 0:
  9.6 31.1 all-gather.9
  318.5 119.5 all-reduce.75
  439.7 28.6 all-gather.11
  491.4 119.5 all-reduce.77
  929.8 74.2 reduce-scatter.16
  1007.6 73.3 reduce-scatter.22
  1084.6 73.2 reduce-scatter.14
  1162.1 128.2 reduce-scatter.24
  1294.7 128.2 reduce-scatter.26
  1427.1 128.2 reduce-scatter.28
  1559.3 61.2 reduce-scatter.32
  1624.4 61.5 reduce-scatter.18
  1689.8 61.5 reduce-scatter.20
  1754.2 67.4 all-reduce.79
  1824.7 37.9 reduce-scatter.30
  1865.3 44.3 all-gather.15
  1911.8 42.6 all-gather.17
  1956.5 42.5 all-gather.13
  2001.3 62.9 all-gather.19
  2066.3 63.3 all-gather.21
  2131.9 63.3 all-gather.23
where the time goes:
time: 2230 us; the launch traced here: 2210 us
  waiting for transfers between devices  1160 us (52%)
  local copies, waits for them, and re-layouts  501 us (22%)
  other arithmetic  236 us (11%)
  blocking collectives  153 us (7%)
  matrix products  138 us (6%)
    slice x66, local copies, waits for them, and re-layouts, body(): lax.associative_scan(combine, (keep_next, d_state), reverse=True)[1]  185 us
    slice x60, local copies, waits for them, and re-layouts, body(): state = lax.associative_scan(combine, (keep, drive))[1]  131 us
    reduce_scatter x1, waiting for transfers between devices, body(): lax.psum_scatter(ffn_gate_grad, 'dp', scatter_dimension=0, tiled=True)  131 us
    reduce_scatter x1, waiting for transfers between devices, body(): lax.psum_scatter(ffn_up_grad, 'dp', scatter_dimension=0, tiled=True)  131 us
    reduce_scatter x1, waiting for transfers between devices, body(): lax.psum_scatter(ffn_down_grad, 'dp', scatter_dimension=1, tiled=True)  130 us
    psum x1, waiting for transfers between devices, body(): resid = whole_in + lax.psum(partial_value, 'tensor')  119 us
    reduce_scatter x1, waiting for transfers between devices, body(): lax.psum_scatter(gate_weight_grad, 'dp', scatter_dimension=0, tiled=True)  75.1 us
    reduce_scatter x1, waiting for transfers between devices, body(): lax.psum_scatter(out_weight_grad, 'dp', scatter_dimension=0, tiled=True)  73.1 us
  transfers between devices with their start and end apart: 21, of which 18 were waited for; matrix products, arithmetic and copies ran while one was open for 11% of the time, Pallas kernels for 0%

commit v1 on v0

v1 whole, which is shorter than its diff:
```python
import functools

import jax
import jax.numpy as jnp
from jax import lax
from jax.experimental import pallas as pl
from jax.experimental.pallas import tpu as pltpu
from jax.sharding import PartitionSpec as P

EPSILON = 1e-06
FLOOR = 0.05
F32 = jnp.float32
BF16 = jnp.bfloat16
LANES = 128
SPAN = 32
HALO = 8
MIB = 1024 * 1024


def params(mib, **more):
    return pltpu.CompilerParams(vmem_limit_bytes=mib * MIB, **more)


def gelu_parts(v):
    c0 = 0.7978845608028654
    c1 = 0.044715
    t = jnp.tanh(c0 * (v + c1 * v * v * v))
    act = 0.5 * v * (1.0 + t)
    slope = 0.5 * (1.0 + t) + 0.5 * v * (1.0 - t * t) * c0 * (1.0 + 3.0 * c1 * v * v)
    return act, slope


def sigmoid(v):
    return 0.5 * jnp.tanh(0.5 * v) + 0.5


def shift_down(v, amount, fill):
    row = lax.broadcasted_iota(jnp.int32, v.shape, 0)
    return jnp.where(row >= amount, pltpu.roll(v, amount, 0), fill)


def shift_up(v, amount, fill):
    row = lax.broadcasted_iota(jnp.int32, v.shape, 0)
    size = v.shape[0]
    return jnp.where(row < size - amount, pltpu.roll(v, size - amount, 0), fill)


def scale_of(decayed, reset):
    rest = 1.0 - decayed * decayed
    return jnp.where(reset, 1.0, jnp.sqrt(jnp.maximum(rest, FLOOR))), rest


def forward_kernel(
    gate_ref, branch_ref, mask_ref, row_ref, rate_w, input_w,
    conv_out, rate_out, open_out, state_out, mixed_out, padded, keep_s, local_s,
):
    tokens = gate_ref.shape[0]
    step = 128
    spans = tokens // SPAN
    padded[0:HALO, :] = jnp.zeros((HALO, LANES), F32)
    padded[HALO:, :] = branch_ref[...]
    wr = rate_w[0]
    wi = input_w[0]

    def fill(i, carry):
        r0 = pl.multiple_of(i * step, step)
        here = pl.ds(r0, step)
        wide = padded[pl.ds(r0, step + HALO), :]
        total = row_ref[4:5, :] + row_ref[0:1, :] * wide[HALO:, :]
        for k in range(1, 4):
            total = total + row_ref[k : k + 1, :] * wide[HALO - k : HALO - k + step, :] * mask_ref[here, k : k + 1]
        low = total.astype(BF16)
        rate = sigmoid(jnp.dot(low, wr, preferred_element_type=F32) + row_ref[5:6, :])
        opened = sigmoid(jnp.dot(low, wi, preferred_element_type=F32) + row_ref[6:7, :])
        reset = mask_ref[here, 0:1] > 0.5
        decayed = jnp.exp(-8.0 * rate * row_ref[7:8, :])
        scale, _ = scale_of(decayed, reset)
        conv_out[here, :] = total
        rate_out[here, :] = rate
        open_out[here, :] = opened
        keep_s[here, :] = jnp.where(reset, 0.0, decayed)
        state_out[here, :] = scale * opened * total
        return carry

    lax.fori_loop(0, tokens // step, fill, 0)
    h = jnp.zeros((spans, LANES), F32)
    p = jnp.ones((spans, LANES), F32)
    for k in range(SPAN):
        at = pl.ds(k, spans, stride=SPAN)
        a = keep_s[at, :]
        h = a * h + state_out[at, :]
        p = p * a
        local_s[at, :] = h
        keep_s[at, :] = p
    jump = 1
    while jump < spans:
        h = h + p * shift_down(h, jump, 0.0)
        p = p * shift_down(p, jump, 1.0)
        jump *= 2
    carry_in = shift_down(h, 1, 0.0)
    for k in range(SPAN):
        at = pl.ds(k, spans, stride=SPAN)
        state_out[at, :] = local_s[at, :] + keep_s[at, :] * carry_in

    def mix(i, carry):
        here = pl.ds(pl.multiple_of(i * step, step), step)
        act, _ = gelu_parts(gate_ref[here, :])
        mixed_out[here, :] = (act * state_out[here, :]).astype(BF16)
        return carry

    lax.fori_loop(0, tokens // step, mix, 0)


def forward_block(gate_pre, branch_pre, masks, rows, rate_weight, input_weight):
    tokens, channels = gate_pre.shape
    heads = rate_weight.shape[0]
    col = pl.BlockSpec((tokens, LANES), lambda h: (0, h))
    whole = pl.BlockSpec(masks.shape, lambda h: (0, 0))
    table = pl.BlockSpec((8, LANES), lambda h: (0, h))
    square = pl.BlockSpec((1, LANES, LANES), lambda h: (h, 0, 0))
    full = jax.ShapeDtypeStruct((tokens, channels), F32)
    return pl.pallas_call(
        forward_kernel,
        grid=(heads,),
        in_specs=[col, col, whole, table, square, square],
        out_specs=[col] * 5,
        out_shape=[full] * 4 + [jax.ShapeDtypeStruct((tokens, channels), BF16)],
        scratch_shapes=[
            pltpu.VMEM((tokens + HALO, LANES), F32),
            pltpu.VMEM((tokens, LANES), F32),
            pltpu.VMEM((tokens, LANES), F32),
        ],
        compiler_params=params(24),
        cost_estimate=pl.CostEstimate(flops=tokens * channels * 700, bytes_accessed=tokens * channels * 26, transcendentals=tokens * channels * 5),
        name="recurrence_forward",
    )(gate_pre, branch_pre, masks, rows, rate_weight, input_weight)


def column_total(v):
    return jnp.sum(v, axis=0, keepdims=True)


def backward_kernel(
    dmix_ref, gate_ref, branch_ref, conv_ref, rate_ref, open_ref, state_ref, mask_ref, row_ref, rate_w, input_w,
    dgate_out, dbranch_out, misc_out, padded, keep_s, adj_s, dconv_s, prev_s, rate_g, input_g, small_g,
):
    tokens = gate_ref.shape[0]
    step = 128
    count = tokens // step
    spans = tokens // SPAN
    zero_halo = jnp.zeros((HALO, LANES), F32)
    padded[0:HALO, :] = zero_halo
    padded[HALO:, :] = branch_ref[...]
    prev_s[0:HALO, :] = zero_halo
    prev_s[HALO:, :] = state_ref[...]
    keep_s[tokens:, :] = zero_halo
    dconv_s[tokens:, :] = zero_halo
    wr = rate_w[0]
    wi = input_w[0]

    def fill(i, total):
        here = pl.ds(pl.multiple_of(i * step, step), step)
        act, slope = gelu_parts(gate_ref[here, :])
        dmix = dmix_ref[here, :]
        dgate = (dmix * state_ref[here, :] * slope).astype(BF16)
        dgate_out[here, :] = dgate
        adj_s[here, :] = dmix * act
        reset = mask_ref[here, 0:1] > 0.5
        keep_s[here, :] = jnp.where(reset, 0.0, jnp.exp(-8.0 * rate_ref[here, :] * row_ref[7:8, :]))
        return total + column_total(dgate.astype(F32))

    gate_bias = lax.fori_loop(0, count, fill, jnp.zeros((1, LANES), F32))
    h = jnp.zeros((spans, LANES), F32)
    p = jnp.ones((spans, LANES), F32)
    for k in reversed(range(SPAN)):
        at = pl.ds(k, spans, stride=SPAN)
        a = keep_s[pl.ds(k + 1, spans, stride=SPAN), :]
        h = a * h + adj_s[at, :]
        p = p * a
        adj_s[at, :] = h
        dconv_s[at, :] = p
    jump = 1
    while jump < spans:
        h = h + p * shift_up(h, jump, 0.0)
        p = p * shift_up(p, jump, 1.0)
        jump *= 2
    carry_in = shift_up(h, 1, 0.0)
    for k in range(SPAN):
        at = pl.ds(k, spans, stride=SPAN)
        adj_s[at, :] = adj_s[at, :] + dconv_s[at, :] * carry_in

    nothing = jnp.zeros((1, LANES), F32)
    rate_g[...] = jnp.zeros_like(rate_g)
    input_g[...] = jnp.zeros_like(input_g)

    def gates(i, totals):
        r0 = pl.multiple_of(i * step, step)
        here = pl.ds(r0, step)
        adj = adj_s[here, :]
        conv = conv_ref[here, :]
        rate = rate_ref[here, :]
        opened = open_ref[here, :]
        reset = mask_ref[here, 0:1] > 0.5
        decay_row = row_ref[7:8, :]
        decayed = jnp.exp(-8.0 * rate * decay_row)
        scale, rest = scale_of(decayed, reset)
        before = prev_s[pl.ds(r0, step + HALO), :][HALO - 1 : HALO - 1 + step, :]
        pull = jnp.where(rest > FLOOR, 1.0, jnp.where(rest == FLOOR, 0.5, 0.0))
        d_scale = adj * opened * conv
        d_decayed = jnp.where(reset, 0.0, adj * before - d_scale * pull * decayed / scale)
        d_log = d_decayed * decayed * -8.0
        d_rate = (d_log * decay_row * rate * (1.0 - rate)).astype(BF16)
        d_input = (adj * scale * conv * opened * (1.0 - opened)).astype(BF16)
        d_conv = (
            adj * scale * opened
            + lax.dot_general(d_rate, wr, (((1,), (1,)), ((), ())), preferred_element_type=F32)
            + lax.dot_general(d_input, wi, (((1,), (1,)), ((), ())), preferred_element_type=F32)
        )
        dconv_s[here, :] = d_conv
        low = conv.astype(BF16)
        rate_g[...] += lax.dot_general(low, d_rate, (((0,), (0,)), ((), ())), preferred_element_type=F32)
        input_g[...] += lax.dot_general(low, d_input, (((0,), (0,)), ((), ())), preferred_element_type=F32)
        wide = padded[pl.ds(r0, step + HALO), :]
        news = [
            column_total(d_conv * wide[HALO:, :]),
            *[
                column_total(d_conv * mask_ref[here, k : k + 1] * wide[HALO - k : HALO - k + step, :])
                for k in range(1, 4)
            ],
            column_total(d_conv),
            column_total(d_rate.astype(F32)),
            column_total(d_input.astype(F32)),
            column_total(d_log * rate),
        ]
        return tuple(t + n for t, n in zip(totals, news))

    totals = lax.fori_loop(0, count, gates, (nothing,) * 8)

    def conv_back(i, total):
        r0 = pl.multiple_of(i * step, step)
        here = pl.ds(r0, step)
        wide = dconv_s[pl.ds(r0, step + HALO), :]
        d_branch = row_ref[0:1, :] * wide[:step, :]
        for k in range(1, 4):
            part = wide * mask_ref[pl.ds(r0, step + HALO), k : k + 1]
            d_branch = d_branch + row_ref[k : k + 1, :] * part[k : k + step, :]
        low = d_branch.astype(BF16)
        dbranch_out[here, :] = low
        return total + column_total(low.astype(F32))

    branch_bias = lax.fori_loop(0, count, conv_back, nothing)
    small_g[...] = jnp.zeros_like(small_g)
    for at, value in enumerate((*totals, gate_bias, branch_bias)):
        small_g[at : at + 1, :] = value
    misc_out[...] = jnp.zeros_like(misc_out)
    misc_out[0:LANES, :] = rate_g[...].astype(BF16)
    misc_out[LANES : 2 * LANES, :] = input_g[...].astype(BF16)
    misc_out[2 * LANES : 2 * LANES + 16, :] = small_g[...].astype(BF16)


def backward_block(d_mixed, gate_pre, branch_pre, conv, rate, opened, state, masks, rows, rate_weight, input_weight):
    tokens, channels = gate_pre.shape
    heads = rate_weight.shape[0]
    col = pl.BlockSpec((tokens, LANES), lambda h: (0, h))
    whole = pl.BlockSpec(masks.shape, lambda h: (0, 0))
    table = pl.BlockSpec((8, LANES), lambda h: (0, h))
    square = pl.BlockSpec((1, LANES, LANES), lambda h: (h, 0, 0))
    misc = pl.BlockSpec((3 * LANES, LANES), lambda h: (0, h))
    return pl.pallas_call(
        backward_kernel,
        grid=(heads,),
        in_specs=[col] * 7 + [whole, table, square, square],
        out_specs=[col, col, misc],
        out_shape=[
            jax.ShapeDtypeStruct((tokens, channels), BF16),
            jax.ShapeDtypeStruct((tokens, channels), BF16),
            jax.ShapeDtypeStruct((3 * LANES, channels), BF16),
        ],
        scratch_shapes=[
            pltpu.VMEM((tokens + HALO, LANES), F32),
            pltpu.VMEM((tokens + HALO, LANES), F32),
            pltpu.VMEM((tokens, LANES), F32),
            pltpu.VMEM((tokens + HALO, LANES), F32),
            pltpu.VMEM((tokens + HALO, LANES), F32),
            pltpu.VMEM((LANES, LANES), F32),
            pltpu.VMEM((LANES, LANES), F32),
            pltpu.VMEM((16, LANES), F32),
        ],
        compiler_params=params(24),
        cost_estimate=pl.CostEstimate(flops=tokens * channels * 1400, bytes_accessed=tokens * channels * 32, transcendentals=tokens * channels * 5),
        name="recurrence_backward",
    )(d_mixed, gate_pre, branch_pre, conv, rate, opened, state, masks, rows, rate_weight, input_weight)


X_PAIRS = [(0, 2), (2, 0), (1, 3), (3, 1)]
CORE_PAIRS = [(0, 1), (1, 0), (2, 3), (3, 2)]


def swap_x(v):
    return lax.ppermute(v, "tensor", X_PAIRS)


def swap_core(v):
    return lax.ppermute(v, "tensor", CORE_PAIRS)


def place():
    at = lax.axis_index("tensor")
    return at // 2, at % 2


def share_features(v):
    across = swap_x(v)
    return v, swap_core(v), across, swap_core(across)


def join_features(pieces):
    at = lax.axis_index("tensor")
    rows, share = pieces[0].shape
    out = jnp.zeros((rows, share * 4), pieces[0].dtype)
    for distance, piece in enumerate(pieces):
        out = lax.dynamic_update_slice_in_dim(out, piece, (at ^ distance) * share, 1)
    return out


def token_start(tokens):
    x, core = place()
    return (core * 2 + x) * (tokens // 4)


def scatter_tokens(v):
    x, core = place()
    half = v.shape[0] // 2
    mine = lax.dynamic_slice_in_dim(v, core * half, half, 0)
    other = lax.dynamic_slice_in_dim(v, (1 - core) * half, half, 0)
    both = mine + swap_core(other.astype(BF16)).astype(F32)
    quarter = half // 2
    mine = lax.dynamic_slice_in_dim(both, x * quarter, quarter, 0)
    other = lax.dynamic_slice_in_dim(both, (1 - x) * quarter, quarter, 0)
    return mine + swap_x(other.astype(BF16)).astype(F32)


def gather_tokens(v):
    x, core = place()
    block = v.shape[0]
    across = swap_x(v)
    near = swap_core(v)
    far = swap_core(across)
    out = jnp.zeros((block * 4, v.shape[1]), v.dtype)
    for piece, where in (
        (v, core * 2 + x),
        (near, (1 - core) * 2 + x),
        (across, core * 2 + 1 - x),
        (far, (1 - core) * 2 + 1 - x),
    ):
        out = lax.dynamic_update_slice_in_dim(out, piece, where * block, 0)
    return out


def scatter_features(v):
    x, core = place()
    share = v.shape[1] // 4

    def part(at):
        return lax.dynamic_slice_in_dim(v, at * share, share, 1)

    def pair(c):
        return part(x * 2 + c), part((1 - x) * 2 + c)

    mine, other = pair(core)
    send_mine, send_other = pair(1 - core)
    got_mine = swap_core(send_mine.astype(BF16)).astype(F32)
    got_other = swap_core(send_other.astype(BF16)).astype(F32)
    return mine + got_mine, swap_x((other + got_other).astype(BF16))


def tensor_sum(v):
    v = v + swap_core(v)
    return v + swap_x(v)


MESH = pl.DeviceIdType.MESH


def ring_kernel(count, n, *refs):
    ins, extra, refs = refs[:count], refs[count : count + 4], refs[count + 4 :]
    outs, sums, refs = refs[:count], refs[count : count + 2], refs[count + 2 :]
    slots, locals_, refs = refs[:count], refs[count : 2 * count], refs[2 * count :]
    send_sem, recv_sem, load_sem, keep_sem = refs[:4]
    held, core_send, core_recv, x_send, x_recv, own, other, held_sem, share_send, share_recv = (
        refs[4:8], *refs[8:]
    )
    hidden_s, down_s, resid_s, first_s = held
    me = lax.axis_index("dp")
    y = lax.rem(me, 2)
    z = me // 2
    p = jnp.where(y == 0, z, n - 1 - z)

    def device(at):
        return jnp.where(at < n // 2, 2 * at, 2 * (n - 1 - at) + 1)

    after, before = device(lax.rem(p + 1, n)), device(lax.rem(p + n - 1, n))
    targets = (after, before)
    at = lax.axis_index("tensor")
    core = lax.rem(at, 2)
    x = at // 2
    core_peer = x * 2 + 1 - core
    x_peer = (1 - x) * 2 + core
    barrier = pltpu.get_barrier_semaphore()
    for target in targets:
        pl.semaphore_signal(barrier, inc=1, device_id={"dp": target}, device_id_type=MESH)
    for target in (core_peer, x_peer):
        pl.semaphore_signal(barrier, inc=1, device_id={"tensor": target}, device_id_type=MESH)
    pl.semaphore_wait(barrier, 4)

    def hold(i):
        return pltpu.make_async_copy(extra[i], held[i], held_sem.at[i])

    for i in range(4):
        hold(i).start()
    tokens, share = own.shape[1:]
    block = tokens // 4

    def share_copy(kind, i):
        if i < 2:
            source, target, device = core_send.at[kind, i], core_recv.at[kind, i], core_peer
        else:
            source, target, device = x_send.at[kind], x_recv.at[kind], x_peer
        return pltpu.make_async_remote_copy(
            source, target, share_send.at[kind, i], share_recv.at[kind, i],
            device_id={"tensor": device}, device_id_type=MESH,
        )

    def output_term(b, rows, cols):
        mine = jnp.where(b == core * 2 + x, 1.0, 0.0)
        return jnp.dot(hidden_s[rows, :], down_s[:, cols], preferred_element_type=F32) + mine * resid_s[:, cols]

    def first_term(b, rows, cols):
        return first_s[rows, cols]

    def share_terms(kind, term):
        def run(b, carry):
            rows = pl.ds(pl.multiple_of(b * block, block), block)
            for xx, c, ref in (
                (1 - x, 1 - core, core_send.at[kind, 1]),
                (x, 1 - core, core_send.at[kind, 0]),
                (1 - x, core, other.at[kind]),
                (x, core, own.at[kind]),
            ):
                cols = pl.ds(pl.multiple_of((xx * 2 + c) * share, LANES), share)
                ref[rows, :] = term(b, rows, cols).astype(ref.dtype)
            return carry

        lax.fori_loop(0, 4, run, 0)
        share_copy(kind, 1).start()
        share_copy(kind, 0).start()

    def share_forward(kind):
        share_copy(kind, 1).wait_recv()
        x_send[kind] = (other[kind] + core_recv[kind, 1].astype(F32)).astype(BF16)
        share_copy(kind, 2).start()

    def share_finish(kind):
        share_copy(kind, 0).wait_recv()
        share_copy(kind, 2).wait_recv()
        total = own[kind] + core_recv[kind, 0].astype(F32) + x_recv[kind].astype(F32)
        sums[kind][...] = total.astype(sums[kind].dtype)

    def piece(ref, q, side, chunk):
        rows = ref.shape[0] // (2 * n)
        start = pl.multiple_of((2 * lax.rem(chunk + n, n) + side) * rows, 8)
        return ref.at[pl.ds(start, rows), :]

    def arriving(side, s):
        if s < n - 1:
            return p - 1 - s if side == 0 else p + 1 + s
        s -= n - 1
        return p - s if side == 0 else p + s

    def send(q, side, s, source):
        if s < n - 1:
            target = slots[q].at[s, side]
        else:
            chunk = p + 1 - (s - n + 1) if side == 0 else p - 1 + (s - n + 1)
            target = piece(outs[q], q, side, chunk + n)
        copy = pltpu.make_async_remote_copy(
            source, target, send_sem.at[q, side, s], recv_sem.at[q, side, s],
            device_id={"dp": targets[side]}, device_id_type=MESH,
        )
        copy.start()

    def wait(q, side, s, which):
        if s < n - 1:
            shape = slots[q].at[s, side]
        else:
            shape = piece(outs[q], q, side, arriving(side, s) + n)
        copy = pltpu.make_async_remote_copy(
            shape, shape, send_sem.at[q, side, s], recv_sem.at[q, side, s],
            device_id={"dp": targets[side]}, device_id_type=MESH,
        )
        (copy.wait_recv if which else copy.wait_send)()

    def load(q, side, s):
        return pltpu.make_async_copy(
            piece(ins[q], q, side, arriving(side, s) + n), locals_[q].at[s % 2, side], load_sem.at[q, side, s % 2]
        )

    for q in range(count):
        for side in range(2):
            send(q, side, 0, piece(ins[q], q, side, p + n))
    for q in range(count):
        for side in range(2):
            load(q, side, 0).start()
    for i in range(4):
        hold(i).wait()
    share_terms(0, output_term)
    share_terms(1, first_term)
    for s in range(n - 1):
        if s == 1:
            share_forward(0)
            share_forward(1)
        if s == 4:
            share_finish(0)
            share_finish(1)
        for q in range(count):
            for side in range(2):
                if s + 1 < n - 1:
                    load(q, side, s + 1).start()
                load(q, side, s).wait()
                wait(q, side, s, True)
                slot = slots[q].at[s, side]
                slot[...] = (slot[...].astype(F32) + locals_[q][s % 2, side].astype(F32)).astype(BF16)
                send(q, side, s + 1, slot)
                if s == n - 2:
                    chunk = p + 1 if side == 0 else p - 1
                    pltpu.make_async_copy(slot, piece(outs[q], q, side, chunk + n), keep_sem.at[q, side]).start()
    for s in range(n - 1, 2 * n - 2):
        for q in range(count):
            for side in range(2):
                wait(q, side, s, True)
                if s + 1 < 2 * n - 2:
                    send(q, side, s + 1, piece(outs[q], q, side, arriving(side, s) + n))
    for q in range(count):
        for side in range(2):
            slot = slots[q].at[n - 2, side]
            chunk = p + 1 if side == 0 else p - 1
            pltpu.make_async_copy(slot, piece(outs[q], q, side, chunk + n), keep_sem.at[q, side]).wait()
            for s in range(2 * n - 2):
                wait(q, side, s, False)
    for kind in range(2):
        for i in range(3):
            share_copy(kind, i).wait_send()


def ring_all(arrays, hidden, down, resid, first):
    n = 8
    count = len(arrays)
    halves = [(a.shape[0] // (2 * n), a.shape[1]) for a in arrays]
    size = sum(a.size for a in arrays)
    extra = (hidden, down, resid, first)
    tokens = hidden.shape[0]
    share = down.shape[1] // 4
    hbm = pl.BlockSpec(memory_space=pl.ANY)
    out = pl.pallas_call(
        functools.partial(ring_kernel, count, n),
        in_specs=[hbm] * (count + 4),
        out_specs=[hbm] * count + [pl.BlockSpec(memory_space=pltpu.VMEM)] * 2,
        out_shape=[
            *[jax.ShapeDtypeStruct(a.shape, BF16) for a in arrays],
            jax.ShapeDtypeStruct((tokens, share), BF16),
            jax.ShapeDtypeStruct((tokens, share), F32),
        ],
        scratch_shapes=[
            *[pltpu.VMEM((n - 1, 2, *h), BF16) for h in halves],
            *[pltpu.VMEM((2, 2, *h), BF16) for h in halves],
            pltpu.SemaphoreType.DMA((count, 2, 2 * n - 2)),
            pltpu.SemaphoreType.DMA((count, 2, 2 * n - 2)),
            pltpu.SemaphoreType.DMA((count, 2, 2)),
            pltpu.SemaphoreType.DMA((count, 2)),
            *[pltpu.VMEM(a.shape, a.dtype) for a in extra],
            pltpu.VMEM((2, 2, tokens, share), BF16),
            pltpu.VMEM((2, 2, tokens, share), BF16),
            pltpu.VMEM((2, tokens, share), BF16),
            pltpu.VMEM((2, tokens, share), BF16),
            pltpu.VMEM((2, tokens, share), F32),
            pltpu.VMEM((2, tokens, share), F32),
            pltpu.SemaphoreType.DMA((4,)),
            pltpu.SemaphoreType.DMA((2, 3)),
            pltpu.SemaphoreType.DMA((2, 3)),
        ],
        compiler_params=params(60, collective_id=0, has_side_effects=True),
        cost_estimate=pl.CostEstimate(flops=2 * size, bytes_accessed=100 * size, transcendentals=0),
        name="ring_all",
    )(*arrays, *extra)
    return out[:count], out[count], out[count + 1]


def dp_sum(arrays, n):
    return [
        lax.all_gather(
            lax.psum_scatter(a, "dp", scatter_dimension=0, tiled=True).astype(BF16), "dp", axis=0, tiled=True
        ).astype(F32)
        if a.shape[0] % n == 0
        else lax.psum(a, "dp")
        for a in arrays
    ]


PIECES = 4


def exchange(tokens, features, product, finish, fill_one, fill_two, out, scratch):
    core_send, core_recv, part, x_send, x_recv, low_send, send_sem, recv_sem, keep_sem = scratch
    at = lax.axis_index("tensor")
    core = lax.rem(at, 2)
    x = at // 2
    core_peer = x * 2 + 1 - core
    x_peer = (1 - x) * 2 + core
    block = tokens // 4
    rows = block // PIECES
    wide = features // 3
    barrier = pltpu.get_barrier_semaphore()
    for target in (core_peer, x_peer):
        pl.semaphore_signal(barrier, inc=1, device_id={"tensor": target}, device_id_type=MESH)
    pl.semaphore_wait(barrier, 2)

    def copy(kind, j, source, target, device):
        return pltpu.make_async_remote_copy(
            source, target, send_sem.at[kind, j], recv_sem.at[kind, j],
            device_id={"tensor": device}, device_id_type=MESH,
        )

    def place_of(c, xx, j):
        return pl.ds(pl.multiple_of((c * 2 + xx) * block + j * rows, rows), rows)

    def piece(j):
        return pl.ds(j * rows, rows)

    def term(c, xx, ref, kind):
        here = pl.ds(pl.multiple_of((c * 2 + xx) * block, block), block)
        for n in range(3):
            cols = pl.ds(n * wide, wide)
            ref[kind, :, cols] = product(here, cols).astype(ref.dtype)

    def core_copy(kind, j):
        return copy(kind, j, core_send.at[kind, piece(j)], core_recv.at[kind, piece(j)], core_peer)

    def x_copy(j):
        return copy(2, j, x_send.at[piece(j)], x_recv.at[piece(j)], x_peer)

    def low_copy(kind, j, c, xx, device):
        return copy(kind, j, low_send.at[piece(j)], out.at[place_of(c, xx, j)], device)

    def relay(j, c, xx):
        return copy(5, j, out.at[place_of(c, xx, j)], out.at[place_of(c, xx, j)], core_peer)

    def keep(j):
        return pltpu.make_async_copy(low_send.at[piece(j)], out.at[place_of(core, x, j)], keep_sem.at[j])

    term(1 - core, 1 - x, core_send, 0)
    for j in range(PIECES):
        core_copy(0, j).start()
    term(core, 1 - x, part, 0)
    for j in range(PIECES):
        core_copy(0, j).wait_recv()
        x_send[piece(j), :] = (part[0, piece(j), :] + core_recv[0, piece(j), :].astype(F32)).astype(BF16)
        x_copy(j).start()
    term(1 - core, x, core_send, 1)
    for j in range(PIECES):
        core_copy(1, j).start()
    term(core, x, part, 1)
    fill_one()
    for j in range(PIECES):
        core_copy(1, j).wait_recv()
        x_copy(j).wait_recv()
        here = piece(j)
        total = part[1, here, :] + core_recv[1, here, :].astype(F32) + x_recv[here, :].astype(F32)
        low_send[here, :] = finish(here, total)
        low_copy(3, j, core, x, x_peer).start()
        low_copy(4, j, core, x, core_peer).start()
        keep(j).start()
    fill_two()
    for j in range(PIECES):
        low_copy(3, j, core, 1 - x, x_peer).wait_recv()
        relay(j, core, 1 - x).start()
    for j in range(PIECES):
        low_copy(4, j, 1 - core, x, core_peer).wait_recv()
        relay(j, 1 - core, 1 - x).wait_recv()
        keep(j).wait()
        core_copy(0, j).wait_send()
        core_copy(1, j).wait_send()
        x_copy(j).wait_send()
        low_copy(3, j, core, x, x_peer).wait_send()
        low_copy(4, j, core, x, core_peer).wait_send()
        relay(j, core, 1 - x).wait_send()


def exchange_scratch(block, features):
    return [
        pltpu.VMEM((2, block, features), BF16),
        pltpu.VMEM((2, block, features), BF16),
        pltpu.VMEM((2, block, features), F32),
        pltpu.VMEM((block, features), BF16),
        pltpu.VMEM((block, features), BF16),
        pltpu.VMEM((block, features), BF16),
        pltpu.SemaphoreType.DMA((6, PIECES)),
        pltpu.SemaphoreType.DMA((6, PIECES)),
        pltpu.SemaphoreType.DMA((PIECES,)),
    ]


def project_kernel(mixed_ref, weight_ref, own_ref, gain_ref, two_out, resid_out, *scratch):
    def product(rows, cols):
        return jnp.dot(mixed_ref[rows, :], weight_ref[:, cols], preferred_element_type=F32)

    def finish(rows, total):
        resid = own_ref[rows, :].astype(F32) + total
        resid_out[rows, :] = resid
        return (resid * rsqrt_mean(resid) * gain_ref[...]).astype(BF16)

    def nothing():
        return None

    exchange(mixed_ref.shape[0], weight_ref.shape[1], product, finish, nothing, nothing, two_out, scratch)


def project(mixed_low, out_weight, own, gain):
    tokens = mixed_low.shape[0]
    features = out_weight.shape[1]
    block = tokens // 4
    return pl.pallas_call(
        project_kernel,
        in_specs=[pl.BlockSpec(memory_space=pltpu.VMEM)] * 4,
        out_specs=[pl.BlockSpec(memory_space=pl.ANY), pl.BlockSpec(memory_space=pltpu.VMEM)],
        out_shape=[
            jax.ShapeDtypeStruct((tokens, features), BF16),
            jax.ShapeDtypeStruct((block, features), F32),
        ],
        scratch_shapes=exchange_scratch(block, features),
        compiler_params=params(22, collective_id=1, has_side_effects=True),
        cost_estimate=pl.CostEstimate(flops=2 * mixed_low.size * features, bytes_accessed=tokens * features * 80, transcendentals=0),
        name="project",
    )(mixed_low, out_weight, own, gain)


def pull_kernel(
    gate_ref, up_ref, gate_w, up_w, two_ref, resid_ref, cot_ref, gain_ref,
    low_out, gain_out, gate_grad, up_grad, *scratch,
):
    features = gate_w.shape[0]
    step = 256
    gain_out[...] = jnp.zeros_like(gain_out)

    def product(rows, cols):
        return lax.dot_general(
            gate_ref[rows, :], gate_w[cols, :], (((1,), (1,)), ((), ())), preferred_element_type=F32
        ) + lax.dot_general(up_ref[rows, :], up_w[cols, :], (((1,), (1,)), ((), ())), preferred_element_type=F32)

    def finish(rows, total):
        resid = resid_ref[rows, :]
        q = rsqrt_mean(resid)
        gain_out[...] += column_total(total * resid * q)
        weighed = gain_ref[...] * total
        pulled = q * weighed - resid * q * q * q * jnp.mean(weighed * resid, axis=-1, keepdims=True)
        return (cot_ref[rows, :].astype(F32) + pulled).astype(BF16)

    def weight_grad(source, target):
        def run(n, carry):
            cols = pl.ds(pl.multiple_of(n * step, step), step)
            target[cols, :] = lax.dot_general(
                two_ref[:, cols], source[...], (((0,), (0,)), ((), ())), preferred_element_type=F32
            ).astype(BF16)
            return carry

        def go():
            lax.fori_loop(0, features // step, run, 0)

        return go

    exchange(
        gate_ref.shape[0], features, product, finish,
        weight_grad(gate_ref, gate_grad), weight_grad(up_ref, up_grad), low_out, scratch,
    )


def pull(d_gate, d_up, gate_w, up_w, two_low, resid, cot, gain):
    tokens, hidden = d_gate.shape
    features = gate_w.shape[0]
    block = tokens // 4
    vmem = pl.BlockSpec(memory_space=pltpu.VMEM)
    return pl.pallas_call(
        pull_kernel,
        in_specs=[vmem] * 8,
        out_specs=[pl.BlockSpec(memory_space=pl.ANY), vmem, vmem, vmem],
        out_shape=[
            jax.ShapeDtypeStruct((tokens, features), BF16),
            jax.ShapeDtypeStruct((1, features), F32),
            jax.ShapeDtypeStruct((features, hidden), BF16),
            jax.ShapeDtypeStruct((features, hidden), BF16),
        ],
        scratch_shapes=exchange_scratch(block, features),
        compiler_params=params(46, collective_id=2, has_side_effects=True),
        cost_estimate=pl.CostEstimate(flops=8 * d_gate.size * features, bytes_accessed=tokens * features * 80, transcendentals=0),
        name="pull",
    )(d_gate, d_up, gate_w, up_w, two_low, resid, cot, gain)


def rsqrt_mean(v):
    return lax.rsqrt(jnp.mean(v * v, axis=-1, keepdims=True) + EPSILON)


def dot(a, b, left, right):
    return lax.dot_general(a, b, (((left,), (right,)), ((), ())), preferred_element_type=F32)


def body(
    n_dp,
    inputs,
    segment_ids,
    cotangent,
    first_gain,
    gate_weight,
    gate_bias,
    branch_weight,
    branch_bias,
    conv_weight,
    conv_bias,
    rate_weight,
    rate_bias,
    input_weight,
    input_bias,
    decay_param,
    out_weight,
    second_gain,
    ffn_gate,
    ffn_up,
    ffn_down,
):
    tokens, share = inputs.shape
    features = share * 4
    channels = gate_weight.shape[1]
    gain_one = first_gain.astype(F32)
    gain_two = second_gain.astype(F32)
    at = lax.axis_index("tensor")
    start = token_start(tokens)
    block = tokens // 4

    row = jnp.arange(tokens, dtype=jnp.int32)
    masks = []
    for k in range(4):
        offset = max(k, 1)
        earlier = jnp.concatenate([jnp.full((offset,), -1, jnp.int32), segment_ids[:-offset]])
        same = (row >= offset) & (segment_ids == earlier)
        masks.append(same if k else ~same)
    masks = jnp.pad(jnp.stack(masks, axis=1).astype(F32), ((0, HALO), (0, 0)))
    rows = jnp.concatenate(
        [
            conv_weight.astype(F32),
            jnp.concatenate([conv_bias, rate_bias, input_bias]).astype(F32).reshape(3, channels),
            jax.nn.softplus(-decay_param)[None],
        ]
    )

    across, masks, rows, gate_bias, branch_bias, gain_one, gain_two = lax.optimization_barrier(
        (swap_x(inputs), masks, rows, gate_bias.astype(F32), branch_bias.astype(F32), gain_one, gain_two)
    )
    in_pieces = (inputs, swap_core(inputs), across, swap_core(across))
    later_cot, _ = lax.optimization_barrier((cotangent, across))
    cot_across = swap_x(later_cot)
    whole_in = join_features(in_pieces)
    in_f = whole_in.astype(F32)
    q_one = rsqrt_mean(in_f)
    normed_low = lax.optimization_barrier((in_f * q_one * gain_one).astype(BF16))
    gate_pre = dot(normed_low, gate_weight, 1, 0) + gate_bias.astype(F32)
    branch_pre = dot(normed_low, branch_weight, 1, 0) + branch_bias.astype(F32)
    conv, rate, opened, state, mixed_low = forward_block(
        gate_pre, branch_pre, masks, rows, rate_weight, input_weight
    )
    mixed_low, cot_across = lax.optimization_barrier((mixed_low, cot_across))
    whole_cot = join_features((cotangent, swap_core(cotangent), cot_across, swap_core(cot_across)))
    two_low, resid = project(
        mixed_low, out_weight, lax.dynamic_slice_in_dim(whole_in, start, block, 0), gain_two[None]
    )
    d_hidden = dot(whole_cot, ffn_down, 1, 1)
    hidden_gate = dot(two_low, ffn_gate, 1, 0)
    hidden_up = dot(two_low, ffn_up, 1, 0)
    hidden_act, hidden_slope = gelu_parts(hidden_gate)
    hidden_low = (hidden_act * hidden_up).astype(BF16)
    cut = hidden_low.shape[1] * 4 // 9
    down_early = dot(hidden_low[:, :cut], whole_cot, 0, 0)
    down_late = dot(hidden_low[:, cut:], whole_cot, 0, 0)
    d_hgate = (d_hidden * hidden_up * hidden_slope).astype(BF16)
    d_hup = (d_hidden * hidden_act).astype(BF16)
    if n_dp == 8:
        down_early, down_late, d_hgate, d_hup = lax.optimization_barrier(
            (down_early.astype(BF16), down_late.astype(BF16), d_hgate, d_hup)
        )
        down_early = lax.psum(down_early, "dp")
    cot_mine = lax.dynamic_slice_in_dim(whole_cot, start, block, 0)
    d_resid_low, second_gain_grad, ffn_gate_grad, ffn_up_grad = pull(
        d_hgate, d_hup, ffn_gate, ffn_up, two_low, resid, cot_mine, gain_two[None]
    )
    second_gain_grad = second_gain_grad[0]
    out_weight_grad = dot(mixed_low, d_resid_low, 0, 0)
    d_mixed = dot(d_resid_low, out_weight, 1, 1)
    d_gate_low, d_branch_low, misc = backward_block(
        d_mixed, gate_pre, branch_pre, conv, rate, opened, state, masks, rows, rate_weight, input_weight
    )
    if n_dp == 8:
        down_early, down_late, d_gate_low = lax.optimization_barrier((down_early, down_late, d_gate_low))
        down_late = lax.psum(down_late, "dp")
    gate_weight_grad = dot(normed_low, d_gate_low, 0, 0)
    branch_weight_grad = dot(normed_low, d_branch_low, 0, 0)
    first_share = dot(d_gate_low, gate_weight, 1, 1) + dot(d_branch_low, branch_weight, 1, 1)
    product = first_share * in_f
    sums = jnp.concatenate([
        jnp.sum(product * q_one, axis=0), second_gain_grad, jnp.sum(product * gain_one, axis=1)
    ])
    sums = tensor_sum(sums.reshape(-1, LANES)).reshape(-1)
    gains = sums[: 2 * features].reshape(-1, channels)
    mean_one = sums[2 * features :, None] / features
    misc = lax.dynamic_update_slice_in_dim(misc, gains.astype(BF16), 2 * LANES + 16, 0)
    summed = [ffn_gate_grad, ffn_up_grad, gate_weight_grad, branch_weight_grad, out_weight_grad, misc]
    if n_dp == 8:
        summed, output, d_first = ring_all([a.astype(BF16) for a in summed], hidden_low, ffn_down, resid, first_share)
        (*summed, down_late) = lax.optimization_barrier((*summed, down_late))
        summed = [a.astype(F32) for a in (jnp.concatenate([down_early, down_late]), *summed)]
    else:
        summed = dp_sum([jnp.concatenate([down_early, down_late]), *summed], n_dp)
        first_here, first_there = scatter_features(first_share)
        d_first = first_here + first_there.astype(F32)
        ffn_part = dot(hidden_low, ffn_down, 1, 0)
        with_resid = lax.dynamic_slice_in_dim(ffn_part, start, block, 0) + resid
        ffn_part = lax.dynamic_update_slice_in_dim(ffn_part, with_resid, start, 0)
        output_here, output_there = scatter_features(ffn_part)
        output = (output_here + output_there.astype(F32)).astype(BF16)
    ffn_down_grad, ffn_gate_grad, ffn_up_grad, gate_weight_grad, branch_weight_grad, out_weight_grad, misc = summed

    own_in = inputs.astype(F32)
    own_gain = lax.dynamic_slice_in_dim(gain_one, at * share, share, 0)
    input_grad = (
        lax.dynamic_slice_in_dim(d_resid_low, at * share, share, 1).astype(F32)
        + q_one * own_gain * d_first
        - own_in * q_one * q_one * q_one * mean_one
    )
    heads = rate_weight.shape[0]

    def blocks(v):
        return v.reshape(LANES, heads, LANES).transpose(1, 0, 2)

    small = misc[2 * LANES : 2 * LANES + 16]
    gains = misc[2 * LANES + 16 : 2 * LANES + 16 + gains.shape[0]].reshape(2, features)
    decay_grad = -small[7] * jax.nn.sigmoid(-decay_param)
    return (
        output,
        input_grad,
        gains[0],
        gate_weight_grad,
        small[8],
        branch_weight_grad,
        small[9],
        small[0:4],
        small[4],
        blocks(misc[:LANES]),
        small[5],
        blocks(misc[LANES : 2 * LANES]),
        small[6],
        decay_grad,
        out_weight_grad,
        gains[1],
        ffn_gate_grad,
        ffn_up_grad,
        ffn_down_grad,
    )


def solution(mesh):
    in_specs = (
        P("dp", "tensor"),
        P("dp"),
        P("dp", "tensor"),
        P(),
        P(None, "tensor"),
        P("tensor"),
        P(None, "tensor"),
        P("tensor"),
        P(None, "tensor"),
        P("tensor"),
        P("tensor", None, None),
        P("tensor"),
        P("tensor", None, None),
        P("tensor"),
        P("tensor"),
        P("tensor", None),
        P(),
        P(None, "tensor"),
        P(None, "tensor"),
        P("tensor", None),
    )
    out_specs = (
        P("dp", "tensor"),
        P("dp", "tensor"),
        P(),
        P(None, "tensor"),
        P("tensor"),
        P(None, "tensor"),
        P("tensor"),
        P(None, "tensor"),
        P("tensor"),
        P("tensor", None, None),
        P("tensor"),
        P("tensor", None, None),
        P("tensor"),
        P("tensor"),
        P("tensor", None),
        P(),
        P(None, "tensor"),
        P(None, "tensor"),
        P("tensor", None),
    )
    return jax.shard_map(
        functools.partial(body, mesh.shape["dp"]), mesh=mesh, in_specs=in_specs, out_specs=out_specs, check_vma=False
    )
```

time: 2230 us -> 593 us (0.27)
  waiting for transfers between devices: 1160 us -> 12.4 us
  local copies, waits for them, and re-layouts: 501 us -> 35.8 us
  Pallas kernels: 0 us -> 425 us
  other arithmetic: 236 us -> 32.1 us
  blocking collectives: 153 us -> 0 us
  matrix products: 138 us -> 56.8 us
    reduce_scatter x8 -> x0, waiting for transfers between devices: 619 us -> none  [the longest x1 131 us: body(): lax.psum_scatter(ffn_gate_grad, 'dp', scatter_dimension=0, tiled=True)]
    pallas_call x0 -> x5, Pallas kernels: none -> 425 us  [the longest x1 279 us: ring_all(): pl.pallas_call(functools.partial(ring_kernel, count, n), in_specs=[hbm] *...]
    slice x129 -> x4, local copies, waits for them, and re-layouts: 320 us -> 1.21 us  [the longest x1 0.6 us: body(): small[0:4]]
    all_gather x8 -> x0, waiting for transfers between devices: 263 us -> none  [the longest x1 61.7 us: body(): lax.all_gather(pieces[14].astype(jnp.bfloat16), 'dp', axis=0, tiled=True)]
    psum x3 -> x2, waiting for transfers between devices: 223 us -> 0.01 us  [the longest x1 0.01 us: body(): down_early = lax.psum(down_early, 'dp')]
    pad x36 -> x0, local copies, waits for them, and re-layouts: 102 us -> none  [the longest x18 51.2 us: body(): lax.associative_scan(combine, (keep_next, d_state), reverse=True)[1]]
    dot_general x24 -> x13, matrix products: 138 us -> 56.8 us  [dot(): lax.dot_general(a, b, (((left,), (right,)), ((), ())), preferred_element_...]
    all_gather x3 -> x0, blocking collectives: 79.9 us -> none  [the longest x1 30.8 us: body(): lax.all_gather(pieces[9].astype(jnp.bfloat16), 'dp', axis=1, tiled=True)]
  transfers between devices with their start and end apart: 21 -> 10, of which waited for: 18 -> 2; matrix products, arithmetic and copies ran while one was open for 11% -> 8% of each run, Pallas kernels for 0% -> 66%
where the time goes in v1:
time: 593 us; the launch traced here: 584 us
  Pallas kernels  425 us (72%)
  matrix products  56.8 us (10%)
  local copies, waits for them, and re-layouts  35.8 us (6%)
  other arithmetic  32.1 us (5%)
  between operations  15.1 us (3%)
  waiting for transfers between devices  12.4 us (2%)
  starting transfers between devices  6.56 us (1%)
    pallas_call x1, Pallas kernels, ring_all(): pl.pallas_call(functools.partial(ring_kernel, count, n), in_specs=[hbm] *...  279 us
    dot_general x13, matrix products, dot(): lax.dot_general(a, b, (((left,), (right,)), ((), ())), preferred_element_...  56.8 us
    pallas_call x1, Pallas kernels, pull(): pl.pallas_call(pull_kernel, in_specs=[vmem] * 8, out_specs=[pl.BlockSpec(...  50.3 us
    pallas_call x1, Pallas kernels, project(): pl.pallas_call(project_kernel, in_specs=[pl.BlockSpec(memory_space=pltpu....  40.2 us
    pallas_call x1, Pallas kernels, backward_block(): pl.pallas_call(backward_kernel, grid=(heads,), in_specs=[col] * 7 + [whol...  32.8 us
    pallas_call x1, Pallas kernels, forward_block(): pl.pallas_call(forward_kernel, grid=(heads,), in_specs=[col, col, whole,...  22.6 us
    convert_element_type x7, other arithmetic, body(): a.astype(F32)  20.8 us
    unnamed x100, local copies, waits for them, and re-layouts  19.7 us
  transfers between devices with their start and end apart: 10, of which 2 were waited for; matrix products, arithmetic and copies ran while one was open for 8% of the time, Pallas kernels for 66%

profile of v1, /device:TPU:0, one launch (start us, length us, event | category | flops | bytes accessed | tf_op | source)
XLA Modules:
  0.0 583.5 jit_solution(6906033498937803299)
XLA Ops:
  7.8 2.6 collective-permute-start.1
  16.6 12.2 %collective-permute-done.1 = bf16[1024,384]{1,0:T(8,128)(2,1)} collective-permute-done((bf16[1024,384]{1,0:T(8,128)(2,1)}, bf16[1024,384]{1,0:T(8,128)(2,1)}, u32[]{:S(2)}, u32[]{:S(2)}) %collective-permute-start.1) | collective-permute-done | bytes 786464 | tf_op jit(solution)/shard_map/ppermute | solution.py:300
  30.5 1.7 collective-permute-start.3
  37.8 1.8 broadcast_add_fusion.branch_ref
  40.4 1.8 broadcast_add_fusion.1.gate_ref
  42.2 22.6 %recurrence_forward.1 = (f32[1024,512]{1,0:T(8,128)S(1)}, f32[1024,512]{1,0:T(8,128)S(1)}, f32[1024,512]{1,0:T(8,128)S(1)}, f32[1024,512]{1,0:T(8,128)S(1)}, bf16[1024,512]{1,0:T(8,128)(2,1)S(1)}) custom-call(f32[1024,512]{1,0:T(8,128)S(1)} %broadcast_add_fusion.1.gate_ref, f32[1024,512]{1,0:T(8,128)S(1)} %broadcast_add_fusion.branch_ref, ...), custom_call_target="tpu_custom_call" | custom-call | flops 367001600 | bytes 13631488 | tf_op jit(solution)/shard_map/recurrence_forward/pallas_call | solution.py:122
  75.8 1.8 constant_dynamic-slice_fusion
  77.7 40.2 %project.1 = (bf16[1024,1536]{1,0:T(8,128)(2,1)S(1)}, f32[256,1536]{1,0:T(8,128)S(1)}) custom-call(bf16[1024,512]{1,0:T(8,128)(2,1)S(1)} %copy-done.20, bf16[512,1536]{1,0:T(8,128)(2,1)S(1)} %copy-done.18, bf16[256,1536]{1,0:T(8,128)(2,1)S(1)} %get-tuple-element.131.own_ref, f32[1,1536]{1,0:T(1,128)S(1)} %broadcast_in_dim.5.gain_ref), custom_call_target="tpu_custom_call" | custom-call | flops 1610612736 | bytes 125829120 | tf_op jit(solution)/shard_map/project/pallas_call | solution.py:731
  117.9 4.2 fusion.20
  122.2 4.2 fusion.21
  126.4 9.5 %multiply_convert_fusion = (bf16[1024,1152]{1,0:T(8,128)(2,1)}, bf16[1024,1152]{1,0:T(8,128)(2,1)}, bf16[1024,1152]{1,0:T(8,128)(2,1)S(1)}) fusion(f32[1024,1152]{1,0:T(8,128)S(1)} %fusion.20, f32[1024,1152]{1,0:T(8,128)S(1)} %fusion.21, bf16[1024,1536]{1,0:T(8,128)(2,1)S(1)} %constant_dynamic-update-slice_fusion, bf16[1152,1536]{1,0:T(8,128)(2,1)S(1)} %copy-done.29), kind=kOutput, calls=%fused_computation.17 | convolution fusion | flops 3653369856 | bytes 23199744 | tf_op jit(solution)/shard_map/dot_general | solution.py:813
  137.3 3.5 convolution_convert_fusion
  140.8 5.2 convolution_convert_fusion.4
  147.5 1.7 copy-done.25
  149.2 1.7 copy-done.26
  150.9 50.3 %pull.1 = (bf16[1024,1536]{1,0:T(8,128)(2,1)}, f32[1,1536]{1,0:T(1,128)S(1)}, bf16[1536,1152]{1,0:T(8,128)(2,1)}, bf16[1536,1152]{1,0:T(8,128)(2,1)}) custom-call(bf16[1024,1152]{1,0:T(8,128)(2,1)S(1)} %copy-done.26, bf16[1024,1152]{1,0:T(8,128)(2,1)S(1)} %copy-done.25, bf16[1536,1152]{1,0:T(8,128)(2,1)} %gate_w.1, bf16[1536,1152]{1,0:T(8,128)(2,1)} %up_w.1, ...), custom_call_target="tpu_custom_call" | custom-call | flops 14495514624 | bytes 125829120 | tf_op jit(solution)/shard_map/pull/pallas_call | solution.py:791
  201.3 4.3 fusion.22.dmix_ref
  206.7 1.6 copy-done.12
  208.3 32.8 %recurrence_backward.1 = (bf16[1024,512]{1,0:T(8,128)(2,1)S(1)}, bf16[1024,512]{1,0:T(8,128)(2,1)S(1)}, bf16[384,512]{1,0:T(8,128)(2,1)S(1)}) custom-call(f32[1024,512]{1,0:T(8,128)S(1)} %fusion.22.dmix_ref, f32[1024,512]{1,0:T(8,128)S(1)} %copy-done.4, f32[1024,512]{1,0:T(8,128)S(1)} %copy-done.2, f32[1024,512]{1,0:T(8,128)S(1)} %copy-done.6, ...), custom_call_target="tpu_custom_call" | custom-call | flops 734003200 | bytes 16777216 | tf_op jit(solution)/shard_map/recurrence_backward/pallas_call | solution.py:269
  242.9 3.0 convolution_convert_fusion.1.refs_4_
  245.9 6.3 %fusion.23 = f32[1024,1536]{1,0:T(8,128)} fusion(bf16[1024,512]{1,0:T(8,128)(2,1)} %copy-done.22, bf16[1536,512]{1,0:T(8,128)(2,1)} %param.24), kind=kOutput, calls=%fused_computation.73 | convolution fusion | flops 1610612736 | bytes 8912896 | tf_op jit(solution)/shard_map/dot_general | solution.py:813
  252.2 7.1 %multiply_reduce_fusion.1 = (f32[1536]{0:T(1024)S(1)}, f32[1024]{0:T(1024)S(1)}, f32[1024,1536]{1,0:T(8,128)}) fusion(bf16[1024,1536]{1,0:T(8,128)(2,1)} %copy-done.27, f32[1024]{0:T(1024)S(1)} %add_rsqrt_fusion, f32[1536]{0:T(1024)S(1)} %convert_element_type.91, f32[1024,1536]{1,0:T(8,128)} %fusion.23, bf16[1024,512]{1,0:T(8,128)(2,1)S(1)} %get-tuple-element.91, ...), kind=kOutput, calls=%fused_computation.9 | convolution fusion | flops 1621620224 | bytes 18370560 | tf_op jit(solution)/shard_map/dot_general | solution.py:813
  259.7 3.0 convolution_convert_fusion.2.refs_3_
  263.4 3.0 convolution_convert_fusion.3.refs_2_
  267.9 278.7 %ring_all.1 = (bf16[1536,1152]{1,0:T(8,128)(2,1)}, bf16[1536,1152]{1,0:T(8,128)(2,1)}, bf16[1536,512]{1,0:T(8,128)(2,1)}, bf16[1536,512]{1,0:T(8,128)(2,1)}, bf1...) custom-call(bf16[1536,1152]{1,0:T(8,128)(2,1)} %get-tuple-element.80.refs_0_, ...), custom_call_target="tpu_custom_call" | custom-call | flops 12189696 | bytes 609484800 | tf_op jit(solution)/shard_map/ring_all/pallas_call | solution.py:564
  546.7 3.4 multiply_subtract_fusion
  551.5 5.6 convert_element_type.110
  557.0 3.4 convert_element_type.111
  560.5 2.1 convert_element_type.107
  562.6 2.1 convert_element_type.108
  564.7 2.1 convert_element_type.109
  570.0 5.4 maximum_convert_fusion
  (166 shorter events, 39.6 us)
Async XLA Ops:
  7.2 30.6 %copy-start = (bf16[1536,512]{1,0:T(8,128)(2,1)S(1)}, bf16[1536,512]{1,0:T(8,128)(2,1)}, u32[]{:S(2)}) copy-start(bf16[1536,512]{1,0:T(8,128)(2,1)} %param.26) | copy-start | bytes 4718596
  7.2 22.3 %copy-start.31 = (bf16[1024,384]{1,0:T(8,128)(2,1)S(1)}, bf16[1024,384]{1,0:T(8,128)(2,1)}, u32[]{:S(2)}) copy-start(bf16[1024,384]{1,0:T(8,128)(2,1)} %param.20) | copy-start | bytes 2359300
  7.2 238.7 %all-reduce.6.cloned.1.call-start = ((), (), s32[]{:S(2)}) async-start(), calls=%async_computation | async-start | bytes 3145728 | tf_op jit(solution)/shard_map/psum | solution.py:898
  7.3 25.0 %collective-permute-start = (bf16[1024,384]{1,0:T(8,128)(2,1)}, bf16[1024,384]{1,0:T(8,128)(2,1)}, u32[]{:S(2)}, u32[]{:S(2)}) collective-permute-start(bf16[1024,384]{1,0:T(8,128)(2,1)} %param.20), channel_id=1, source_target_pairs={{0,1},{1,0},{2,3},{3,2},{4,5},{5,4},{6,7},{7,6},{8,9},{9,8},{10,11... | collective-permute-start | bytes 2359304 | tf_op jit(solution)/shard_map/ppermute | solution.py:304
  7.8 21.0 %collective-permute-start.1 = (bf16[1024,384]{1,0:T(8,128)(2,1)}, bf16[1024,384]{1,0:T(8,128)(2,1)}, u32[]{:S(2)}, u32[]{:S(2)}) collective-permute-start(bf16[1024,384]{1,0:T(8,128)(2,1)} %param.20), channel_id=1, source_target_pairs={{0,2},{2,0},{1,3},{3,1},{4,6},{6,4},{5,7},{7,5},{8,10},{10,8},{9,1... | collective-permute-start | bytes 2359304 | tf_op jit(solution)/shard_map/ppermute | solution.py:300
  28.8 6.0 %collective-permute-start.2 = (bf16[1024,384]{1,0:T(8,128)(2,1)}, bf16[1024,384]{1,0:T(8,128)(2,1)}, u32[]{:S(2)}, u32[]{:S(2)}) collective-permute-start(bf16[1024,384]{1,0:T(8,128)(2,1)} %collective-permute-done.1), channel_id=1, source_target_pairs={{0,1},{1,0},{2,3},{3,2},{4,5},{5,4},{6,7},{7,6},{8,9},{9,8},{10,11... | collective-permute-start | bytes 2359304 | tf_op jit(solution)/shard_map/ppermute | solution.py:304
  28.8 42.9 %collective-permute-start.4 = (bf16[1024,384]{1,0:T(8,128)(2,1)}, bf16[1024,384]{1,0:T(8,128)(2,1)}, u32[]{:S(2)}, u32[]{:S(2)}) collective-permute-start(bf16[1024,384]{1,0:T(8,128)(2,1)} %param.22), channel_id=1, source_target_pairs={{0,1},{1,0},{2,3},{3,2},{4,5},{5,4},{6,7},{7,6},{8,9},{9,8},{10,11... | collective-permute-start | bytes 2359304 | tf_op jit(solution)/shard_map/ppermute | solution.py:304
  30.5 40.8 %collective-permute-start.3 = (bf16[1024,384]{1,0:T(8,128)(2,1)S(1)}, bf16[1024,384]{1,0:T(8,128)(2,1)}, u32[]{:S(2)}, u32[]{:S(2)}) collective-permute-start(bf16[1024,384]{1,0:T(8,128)(2,1)S(1)} %copy-done.40), channel_id=1, source_target_pairs={{0,2},{2,0},{1,3},{3,1},{4,6},{6,4},{5,7},{7,5},{8,10},{10,8},{9,1... | collective-permute-start | bytes 2359304 | tf_op jit(solution)/shard_map/ppermute | solution.py:300
  42.2 22.6 %copy-start.3 = (f32[1024,512]{1,0:T(8,128)}, f32[1024,512]{1,0:T(8,128)S(1)}, u32[]{:S(2)}) copy-start(f32[1024,512]{1,0:T(8,128)S(1)} %broadcast_add_fusion.1.gate_ref) | copy-start | bytes 6291460
  42.2 29.3 %copy-start.41 = (bf16[1024,384]{1,0:T(8,128)(2,1)S(1)}, bf16[1024,384]{1,0:T(8,128)(2,1)}, u32[]{:S(2)}) copy-start(bf16[1024,384]{1,0:T(8,128)(2,1)} %param.22) | copy-start | bytes 2359300
  71.2 3.3 collective-permute-start.5
  73.0 4.7 copy-start.18
  73.0 4.7 copy-start.20
  75.8 60.1 %copy-start.28 = (bf16[1024,1536]{1,0:T(8,128)(2,1)}, bf16[1024,1536]{1,0:T(8,128)(2,1)S(1)}, u32[]{:S(2)}) copy-start(bf16[1024,1536]{1,0:T(8,128)(2,1)S(1)} %constant_dynamic-update-slice_fusion) | copy-start | bytes 9437188
  77.7 40.3 %copy-start.46 = (bf16[1536,1152]{1,0:T(8,128)(2,1)S(1)}, bf16[1536,1152]{1,0:T(8,128)(2,1)}, u32[]{:S(2)}) copy-start(bf16[1536,1152]{1,0:T(8,128)(2,1)} %gate_w.1) | copy-start | bytes 10616836
  117.9 4.3 copy-start.13
  117.9 4.3 copy-start.24
  146.1 404.0 %all-reduce.8.cloned.1.call-start = ((), (), s32[]{:S(2)}) async-start(), calls=%async_computation.1 | async-start | bytes 3932160 | tf_op jit(solution)/shard_map/psum | solution.py:911
  201.2 4.4 copy-start.2
  201.2 4.4 copy-start.4
  201.2 4.4 copy-start.6
  201.2 4.9 copy-start.8
  201.2 5.5 copy-start.10
  208.3 34.6 %copy-start.21 = (bf16[1024,512]{1,0:T(8,128)(2,1)S(1)}, bf16[1024,512]{1,0:T(8,128)(2,1)}, u32[]{:S(2)}) copy-start(bf16[1024,512]{1,0:T(8,128)(2,1)} %copy-done.19) | copy-start | bytes 3145732
  208.3 34.6 %copy-start.44 = (bf16[1024,1536]{1,0:T(8,128)(2,1)S(1)}, bf16[1024,1536]{1,0:T(8,128)(2,1)}, u32[]{:S(2)}) copy-start(bf16[1024,1536]{1,0:T(8,128)(2,1)} %get-tuple-element.84) | copy-start | bytes 9437188
  252.2 7.6 %copy-start.34 = (bf16[1024,1536]{1,0:T(8,128)(2,1)S(1)}, bf16[1024,1536]{1,0:T(8,128)(2,1)}, u32[]{:S(2)}) copy-start(bf16[1024,1536]{1,0:T(8,128)(2,1)} %copy-done.33) | copy-start | bytes 9437188
  259.3 3.4 collective-permute-start.6
  262.7 3.8 collective-permute-start.7
  267.9 278.8 %copy-start.32 = (bf16[1024,384]{1,0:T(8,128)(2,1)S(1)}, bf16[1024,384]{1,0:T(8,128)(2,1)}, u32[]{:S(2)}) copy-start(bf16[1024,384]{1,0:T(8,128)(2,1)} %param.20) | copy-start | bytes 2359300
  551.5 5.6 copy-start.30
  564.7 5.3 copy-start.36
  570.0 5.4 copy-start.42
  (27 other events, 55.6 us)
Sparse Core Ops, SparseCore 0:
  146.2 89.6 all-reduce.5
  252.3 133.2 all-reduce.7

commit v2 on v1

--- a/solution.py
+++ b/solution.py
@@ -130,7 +130,7 @@
             pltpu.VMEM((tokens, LANES), F32),
             pltpu.VMEM((tokens, LANES), F32),
         ],
-        compiler_params=params(24),
+        compiler_params=params(60),
         cost_estimate=pl.CostEstimate(flops=tokens * channels * 700, bytes_accessed=tokens * channels * 26, transcendentals=tokens * channels * 5),
         name="recurrence_forward",
     )(gate_pre, branch_pre, masks, rows, rate_weight, input_weight)
@@ -286,7 +286,7 @@
             pltpu.VMEM((LANES, LANES), F32),
             pltpu.VMEM((16, LANES), F32),
         ],
-        compiler_params=params(24),
+        compiler_params=params(60),
         cost_estimate=pl.CostEstimate(flops=tokens * channels * 1400, bytes_accessed=tokens * channels * 32, transcendentals=tokens * channels * 5),
         name="recurrence_backward",
     )(d_mixed, gate_pre, branch_pre, conv, rate, opened, state, masks, rows, rate_weight, input_weight)
@@ -380,17 +380,20 @@
 
 
 MESH = pl.DeviceIdType.MESH
-
-
-def ring_kernel(count, n, *refs):
-    ins, extra, refs = refs[:count], refs[count : count + 4], refs[count + 4 :]
+HELD = 9
+
+
+def ring_kernel(given, n, *refs):
+    count = given + 3
+    ins, extra, refs = refs[:given], refs[given : given + HELD], refs[given + HELD :]
     outs, sums, refs = refs[:count], refs[count : count + 2], refs[count + 2 :]
     slots, locals_, refs = refs[:count], refs[count : 2 * count], refs[2 * count :]
     send_sem, recv_sem, load_sem, keep_sem = refs[:4]
-    held, core_send, core_recv, x_send, x_recv, own, other, held_sem, share_send, share_recv = (
-        refs[4:8], *refs[8:]
-    )
-    hidden_s, down_s, resid_s, first_s = held
+    held, refs = refs[4 : 4 + HELD], refs[4 + HELD :]
+    core_send, core_recv, x_send, x_recv, own, other, held_sem, share_send, share_recv = refs[:9]
+    made = refs[9:]
+    ins = (*ins, *made)
+    normed_s, gate_s, branch_s, mixed_s, low_s, hidden_s, down_s, resid_s, first_s = held
     me = lax.axis_index("dp")
     y = lax.rem(me, 2)
     z = me // 2
@@ -416,9 +419,7 @@
     def hold(i):
         return pltpu.make_async_copy(extra[i], held[i], held_sem.at[i])
 
-    for i in range(4):
-        hold(i).start()
-    tokens, share = own.shape[1:]
+    tokens, share = own.shape
     block = tokens // 4
 
     def share_copy(kind, i):
@@ -431,40 +432,52 @@
             device_id={"tensor": device}, device_id_type=MESH,
         )
 
-    def output_term(b, rows, cols):
-        mine = jnp.where(b == core * 2 + x, 1.0, 0.0)
-        return jnp.dot(hidden_s[rows, :], down_s[:, cols], preferred_element_type=F32) + mine * resid_s[:, cols]
-
-    def first_term(b, rows, cols):
-        return first_s[rows, cols]
-
-    def share_terms(kind, term):
-        def run(b, carry):
-            rows = pl.ds(pl.multiple_of(b * block, block), block)
-            for xx, c, ref in (
-                (1 - x, 1 - core, core_send.at[kind, 1]),
-                (x, 1 - core, core_send.at[kind, 0]),
-                (1 - x, core, other.at[kind]),
-                (x, core, own.at[kind]),
-            ):
-                cols = pl.ds(pl.multiple_of((xx * 2 + c) * share, LANES), share)
-                ref[rows, :] = term(b, rows, cols).astype(ref.dtype)
-            return carry
-
-        lax.fori_loop(0, 4, run, 0)
+    def share_cols(xx, c):
+        return pl.ds(pl.multiple_of((xx * 2 + c) * share, LANES), share)
+
+    def output_terms(b):
+        rows = pl.ds(b * block, block)
+        mine = jnp.where(core * 2 + x == b, 1.0, 0.0)
+        for xx, c, ref in (
+            (1 - x, 1 - core, core_send.at[0, 1]),
+            (x, 1 - core, core_send.at[0, 0]),
+            (1 - x, core, other),
+            (x, core, own),
+        ):
+            cols = share_cols(xx, c)
+            term = jnp.dot(hidden_s[rows, :], down_s[:, cols], preferred_element_type=F32) + mine * resid_s[:, cols]
+            ref[rows, :] = term.astype(ref.dtype)
+
+    def first_terms():
+        core_send[1, 1] = first_s[:, share_cols(1 - x, 1 - core)].astype(BF16)
+        core_send[1, 0] = first_s[:, share_cols(x, 1 - core)].astype(BF16)
+
+    def share_start(kind):
         share_copy(kind, 1).start()
         share_copy(kind, 0).start()
 
     def share_forward(kind):
         share_copy(kind, 1).wait_recv()
-        x_send[kind] = (other[kind] + core_recv[kind, 1].astype(F32)).astype(BF16)
+        far = first_s[:, share_cols(1 - x, core)] if kind else other[...]
+        x_send[kind] = (far + core_recv[kind, 1].astype(F32)).astype(BF16)
         share_copy(kind, 2).start()
 
     def share_finish(kind):
         share_copy(kind, 0).wait_recv()
         share_copy(kind, 2).wait_recv()
-        total = own[kind] + core_recv[kind, 0].astype(F32) + x_recv[kind].astype(F32)
+        near = first_s[:, share_cols(x, core)] if kind else own[...]
+        total = near + core_recv[kind, 0].astype(F32) + x_recv[kind].astype(F32)
         sums[kind][...] = total.astype(sums[kind].dtype)
+
+    def weight_grad(source, by, target):
+        def run(i, carry):
+            cols = pl.ds(pl.multiple_of(i * 256, 256), 256)
+            target[cols, :] = lax.dot_general(
+                source[:, cols], by[...], (((0,), (0,)), ((), ())), preferred_element_type=F32
+            ).astype(BF16)
+            return carry
+
+        lax.fori_loop(0, source.shape[1] // 256, run, 0)
 
     def piece(ref, q, side, chunk):
         rows = ref.shape[0] // (2 * n)
@@ -505,24 +518,38 @@
             piece(ins[q], q, side, arriving(side, s) + n), locals_[q].at[s % 2, side], load_sem.at[q, side, s % 2]
         )
 
-    for q in range(count):
+    def begin(q):
         for side in range(2):
             send(q, side, 0, piece(ins[q], q, side, p + n))
-    for q in range(count):
-        for side in range(2):
             load(q, side, 0).start()
-    for i in range(4):
+
+    for q in range(given):
+        begin(q)
+    for i in range(HELD):
+        hold(i).start()
+    for i in range(5):
         hold(i).wait()
-    share_terms(0, output_term)
-    share_terms(1, first_term)
+    for i, (source, by) in enumerate(((normed_s, gate_s), (normed_s, branch_s), (mixed_s, low_s))):
+        weight_grad(source, by, made[i])
+        begin(given + i)
+    for i in range(5, HELD):
+        hold(i).wait()
     for s in range(n - 1):
         if s == 1:
+            share_start(0)
+            first_terms()
+            share_start(1)
+        if s == 2:
             share_forward(0)
+        if s == 3:
             share_forward(1)
-        if s == 4:
+        if s == 5:
             share_finish(0)
+        if s == 6:
             share_finish(1)
         for q in range(count):
+            if s == 0 and q < 4:
+                output_terms(q)
             for side in range(2):
                 if s + 1 < n - 1:
                     load(q, side, s + 1).start()
@@ -552,21 +579,27 @@
             share_copy(kind, i).wait_send()
 
 
-def ring_all(arrays, hidden, down, resid, first):
+def ring_all(arrays, normed, d_gate, d_branch, mixed, low, hidden, down, resid, first):
     n = 8
-    count = len(arrays)
-    halves = [(a.shape[0] // (2 * n), a.shape[1]) for a in arrays]
-    size = sum(a.size for a in arrays)
-    extra = (hidden, down, resid, first)
+    given = len(arrays)
+    made = [
+        jax.ShapeDtypeStruct((a.shape[1], b.shape[1]), BF16)
+        for a, b in ((normed, d_gate), (normed, d_branch), (mixed, low))
+    ]
+    reduced = [*arrays, *made]
+    count = len(reduced)
+    halves = [(a.shape[0] // (2 * n), a.shape[1]) for a in reduced]
+    size = sum(a.size for a in reduced)
+    extra = (normed, d_gate, d_branch, mixed, low, hidden, down, resid, first)
     tokens = hidden.shape[0]
     share = down.shape[1] // 4
     hbm = pl.BlockSpec(memory_space=pl.ANY)
     out = pl.pallas_call(
-        functools.partial(ring_kernel, count, n),
-        in_specs=[hbm] * (count + 4),
+        functools.partial(ring_kernel, given, n),
+        in_specs=[hbm] * (given + HELD),
         out_specs=[hbm] * count + [pl.BlockSpec(memory_space=pltpu.VMEM)] * 2,
         out_shape=[
-            *[jax.ShapeDtypeStruct(a.shape, BF16) for a in arrays],
+            *[jax.ShapeDtypeStruct(a.shape, BF16) for a in reduced],
             jax.ShapeDtypeStruct((tokens, share), BF16),
             jax.ShapeDtypeStruct((tokens, share), F32),
         ],
@@ -582,13 +615,14 @@
             pltpu.VMEM((2, 2, tokens, share), BF16),
             pltpu.VMEM((2, tokens, share), BF16),
             pltpu.VMEM((2, tokens, share), BF16),
-            pltpu.VMEM((2, tokens, share), F32),
-            pltpu.VMEM((2, tokens, share), F32),
-            pltpu.SemaphoreType.DMA((4,)),
+            pltpu.VMEM((tokens, share), F32),
+            pltpu.VMEM((tokens, share), F32),
+            pltpu.SemaphoreType.DMA((HELD,)),
             pltpu.SemaphoreType.DMA((2, 3)),
             pltpu.SemaphoreType.DMA((2, 3)),
+            *[pltpu.VMEM(a.shape, BF16) for a in made],
         ],
-        compiler_params=params(60, collective_id=0, has_side_effects=True),
+        compiler_params=params(63, collective_id=0, has_side_effects=True),
         cost_estimate=pl.CostEstimate(flops=2 * size, bytes_accessed=100 * size, transcendentals=0),
         name="ring_all",
     )(*arrays, *extra)
@@ -901,7 +935,6 @@
         d_hgate, d_hup, ffn_gate, ffn_up, two_low, resid, cot_mine, gain_two[None]
     )
     second_gain_grad = second_gain_grad[0]
-    out_weight_grad = dot(mixed_low, d_resid_low, 0, 0)
     d_mixed = dot(d_resid_low, out_weight, 1, 1)
     d_gate_low, d_branch_low, misc = backward_block(
         d_mixed, gate_pre, branch_pre, conv, rate, opened, state, masks, rows, rate_weight, input_weight
@@ -909,8 +942,6 @@
     if n_dp == 8:
         down_early, down_late, d_gate_low = lax.optimization_barrier((down_early, down_late, d_gate_low))
         down_late = lax.psum(down_late, "dp")
-    gate_weight_grad = dot(normed_low, d_gate_low, 0, 0)
-    branch_weight_grad = dot(normed_low, d_branch_low, 0, 0)
     first_share = dot(d_gate_low, gate_weight, 1, 1) + dot(d_branch_low, branch_weight, 1, 1)
     product = first_share * in_f
     sums = jnp.concatenate([
@@ -920,12 +951,19 @@
     gains = sums[: 2 * features].reshape(-1, channels)
     mean_one = sums[2 * features :, None] / features
     misc = lax.dynamic_update_slice_in_dim(misc, gains.astype(BF16), 2 * LANES + 16, 0)
-    summed = [ffn_gate_grad, ffn_up_grad, gate_weight_grad, branch_weight_grad, out_weight_grad, misc]
     if n_dp == 8:
-        summed, output, d_first = ring_all([a.astype(BF16) for a in summed], hidden_low, ffn_down, resid, first_share)
+        (ffn_gate_grad, ffn_up_grad, misc, *summed), output, d_first = ring_all(
+            [ffn_gate_grad, ffn_up_grad, misc],
+            normed_low, d_gate_low, d_branch_low, mixed_low, d_resid_low, hidden_low, ffn_down, resid, first_share,
+        )
+        summed = [ffn_gate_grad, ffn_up_grad, *summed, misc]
         (*summed, down_late) = lax.optimization_barrier((*summed, down_late))
         summed = [a.astype(F32) for a in (jnp.concatenate([down_early, down_late]), *summed)]
     else:
+        gate_weight_grad = dot(normed_low, d_gate_low, 0, 0)
+        branch_weight_grad = dot(normed_low, d_branch_low, 0, 0)
+        out_weight_grad = dot(mixed_low, d_resid_low, 0, 0)
+        summed = [ffn_gate_grad, ffn_up_grad, gate_weight_grad, branch_weight_grad, out_weight_grad, misc]
         summed = dp_sum([jnp.concatenate([down_early, down_late]), *summed], n_dp)
         first_here, first_there = scatter_features(first_share)
         d_first = first_here + first_there.astype(F32)

time: 593 us -> 585 us (0.987)
  local copies, waits for them, and re-layouts: 35.8 us -> 22.7 us
    unnamed x100 -> x56, local copies, waits for them, and re-layouts: 19.7 us -> 6.75 us
    dot_general x13 -> x10, matrix products: 56.8 us -> 53.3 us  [dot(): lax.dot_general(a, b, (((left,), (right,)), ((), ())), preferred_element_...]
  transfers between devices with their start and end apart: 10 -> 10, of which waited for: 2 -> 4; matrix products, arithmetic and copies ran while one was open for 8% -> 7% of each run, Pallas kernels for 66% -> 68%
where the time goes in v2:
time: 585 us; the launch traced here: 576 us
  Pallas kernels  430 us (74%)
  matrix products  53.3 us (9%)
  other arithmetic  31.3 us (5%)
  local copies, waits for them, and re-layouts  22.7 us (4%)
  waiting for transfers between devices  16.5 us (3%)
  between operations  15 us (3%)
  starting transfers between devices  6.48 us (1%)
    pallas_call x1, Pallas kernels, ring_all(): pl.pallas_call(functools.partial(ring_kernel, given, n), in_specs=[hbm] *...  280 us
    dot_general x10, matrix products, dot(): lax.dot_general(a, b, (((left,), (right,)), ((), ())), preferred_element_...  53.3 us
    pallas_call x1, Pallas kernels, pull(): pl.pallas_call(pull_kernel, in_specs=[vmem] * 8, out_specs=[pl.BlockSpec(...  52.5 us
    pallas_call x1, Pallas kernels, project(): pl.pallas_call(project_kernel, in_specs=[pl.BlockSpec(memory_space=pltpu....  40.2 us
    pallas_call x1, Pallas kernels, backward_block(): pl.pallas_call(backward_kernel, grid=(heads,), in_specs=[col] * 7 + [whol...  34.1 us
    pallas_call x1, Pallas kernels, forward_block(): pl.pallas_call(forward_kernel, grid=(heads,), in_specs=[col, col, whole,...  23.9 us
    convert_element_type x7, other arithmetic, body(): a.astype(F32)  18.2 us
    ppermute x3, waiting for transfers between devices, swap_x(): return lax.ppermute(v, 'tensor', X_PAIRS)  14 us
  transfers between devices with their start and end apart: 10, of which 4 were waited for; matrix products, arithmetic and copies ran while one was open for 7% of the time, Pallas kernels for 68%

profile of v2, /device:TPU:0, one launch (start us, length us, event | category | flops | bytes accessed | tf_op | source)
XLA Modules:
  0.0 575.7 jit_solution(3781471701504758085)
XLA Ops:
  7.8 2.6 collective-permute-start.1
  18.0 10.8 %collective-permute-done.1 = bf16[1024,384]{1,0:T(8,128)(2,1)} collective-permute-done((bf16[1024,384]{1,0:T(8,128)(2,1)}, bf16[1024,384]{1,0:T(8,128)(2,1)}, u32[]{:S(2)}, u32[]{:S(2)}) %collective-permute-start.1) | collective-permute-done | bytes 786464 | tf_op jit(solution)/shard_map/ppermute | solution.py:300
  29.7 1.8 collective-permute-start.3
  38.0 3.1 broadcast_add_fusion.branch_ref
  41.1 3.2 broadcast_add_fusion.1.gate_ref
  44.2 23.9 %recurrence_forward.1 = (f32[1024,512]{1,0:T(8,128)}, f32[1024,512]{1,0:T(8,128)}, f32[1024,512]{1,0:T(8,128)}, f32[1024,512]{1,0:T(8,128)}, bf16[1024,512]{1,0:T(8,128)(2,1)}) custom-call(f32[1024,512]{1,0:T(8,128)} %broadcast_add_fusion.1.gate_ref, f32[1024,512]{1,0:T(8,128)} %broadcast_add_fusion.branch_ref, f32[1032,4]{1,0:T(8,128)} %pad_convert_fusion.mask_ref, ...), custom_call_target="tpu_custom_call" | custom-call | flops 367001600 | bytes 13631488 | tf_op jit(solution)/shard_map/recurrence_forward/pallas_call | solution.py:122
  69.0 1.6 collective-permute-done.5
  72.0 1.8 constant_dynamic-slice_fusion
  73.8 40.2 %project.1 = (bf16[1024,1536]{1,0:T(8,128)(2,1)S(1)}, f32[256,1536]{1,0:T(8,128)S(1)}) custom-call(bf16[1024,512]{1,0:T(8,128)(2,1)S(1)} %copy-done.1, bf16[512,1536]{1,0:T(8,128)(2,1)S(1)} %copy-done.2, bf16[256,1536]{1,0:T(8,128)(2,1)S(1)} %get-tuple-element.131.own_ref, f32[1,1536]{1,0:T(1,128)S(1)} %broadcast_in_dim.5.gain_ref), custom_call_target="tpu_custom_call" | custom-call | flops 1610612736 | bytes 125829120 | tf_op jit(solution)/shard_map/project/pallas_call | solution.py:765
  114.1 4.2 fusion.20
  118.3 4.2 fusion.21
  122.6 9.4 %multiply_convert_fusion = (bf16[1024,1152]{1,0:T(8,128)(2,1)}, bf16[1024,1152]{1,0:T(8,128)(2,1)}, bf16[1024,1152]{1,0:T(8,128)(2,1)S(1)}) fusion(f32[1024,1152]{1,0:T(8,128)S(1)} %fusion.20, f32[1024,1152]{1,0:T(8,128)S(1)} %fusion.21, bf16[1024,1536]{1,0:T(8,128)(2,1)S(1)} %constant_dynamic-update-slice_fusion, bf16[1152,1536]{1,0:T(8,128)(2,1)S(1)} %copy-done.12), kind=kOutput, calls=%fused_computation.17 | convolution fusion | flops 3653369856 | bytes 23199744 | tf_op jit(solution)/shard_map/dot_general | solution.py:847
  132.0 1.4 copy-done.14
  133.4 3.5 convolution_convert_fusion
  136.9 5.2 convolution_convert_fusion.1
  142.2 1.7 copy-done.4
  143.9 1.7 copy-done.5
  145.5 52.5 %pull.1 = (bf16[1024,1536]{1,0:T(8,128)(2,1)}, f32[1,1536]{1,0:T(1,128)S(1)}, bf16[1536,1152]{1,0:T(8,128)(2,1)}, bf16[1536,1152]{1,0:T(8,128)(2,1)}) custom-call(bf16[1024,1152]{1,0:T(8,128)(2,1)S(1)} %copy-done.5, bf16[1024,1152]{1,0:T(8,128)(2,1)S(1)} %copy-done.4, bf16[1536,1152]{1,0:T(8,128)(2,1)} %gate_w.1, bf16[1536,1152]{1,0:T(8,128)(2,1)} %up_w.1, ...), custom_call_target="tpu_custom_call" | custom-call | flops 14495514624 | bytes 125829120 | tf_op jit(solution)/shard_map/pull/pallas_call | solution.py:825
  198.1 5.5 fusion.22.dmix_ref
  203.6 34.1 %recurrence_backward.1 = (bf16[1024,512]{1,0:T(8,128)(2,1)}, bf16[1024,512]{1,0:T(8,128)(2,1)}, bf16[384,512]{1,0:T(8,128)(2,1)}) custom-call(f32[1024,512]{1,0:T(8,128)} %fusion.22.dmix_ref, f32[1024,512]{1,0:T(8,128)} %broadcast_add_fusion.1.gate_ref, f32[1024,512]{1,0:T(8,128)} %broadcast_add_fusion.branch_ref, f32[1024,512]{1,0:T(8,128)} %get-tuple-element.83.conv_ref, ...), custom_call_target="tpu_custom_call" | custom-call | flops 734003200 | bytes 16777216 | tf_op jit(solution)/shard_map/recurrence_backward/pallas_call | solution.py:269
  237.8 6.4 %fusion.23 = f32[1024,1536]{1,0:T(8,128)} fusion(bf16[1024,512]{1,0:T(8,128)(2,1)} %get-tuple-element.91.refs_4_, bf16[1536,512]{1,0:T(8,128)(2,1)} %param.24), kind=kOutput, calls=%fused_computation.70 | convolution fusion | flops 1610612736 | bytes 8912896 | tf_op jit(solution)/shard_map/dot_general | solution.py:847
  244.2 8.5 %multiply_reduce_fusion.1 = (f32[1536]{0:T(1024)S(1)}, f32[1024]{0:T(1024)S(1)}, f32[1024,1536]{1,0:T(8,128)}) fusion(bf16[1024,1536]{1,0:T(8,128)(2,1)S(1)} %copy-done.7, f32[1024]{0:T(1024)S(1)} %add_rsqrt_fusion, f32[1536]{0:T(1024)S(1)} %convert_element_type.82, f32[1024,1536]{1,0:T(8,128)} %fusion.23, bf16[1024,512]{1,0:T(8,128)(2,1)} %get-tuple-element.92.refs_5_, ...), kind=kOutput, calls=%fused_computation.9 | convolution fusion | flops 1621620224 | bytes 18370560 | tf_op jit(solution)/shard_map/dot_general | solution.py:847
  254.5 3.2 collective-permute-done.7
  259.1 279.6 %ring_all.1 = (bf16[1536,1152]{1,0:T(8,128)(2,1)}, bf16[1536,1152]{1,0:T(8,128)(2,1)}, bf16[384,512]{1,0:T(8,128)(2,1)}, bf16[1536,512]{1,0:T(8,128)(2,1)}, bf16...) custom-call(bf16[1536,1152]{1,0:T(8,128)(2,1)} %get-tuple-element.80.refs_0_, ...), custom_call_target="tpu_custom_call" | custom-call | flops 12189696 | bytes 609484800 | tf_op jit(solution)/shard_map/ring_all/pallas_call | solution.py:597
  538.8 3.7 multiply_subtract_fusion
  544.4 1.4 fusion.19
  547.1 3.5 convert_element_type.98
  550.6 3.4 convert_element_type.99
  554.1 2.1 convert_element_type.95
  556.2 2.1 convert_element_type.96
  558.3 2.1 convert_element_type.97
  563.6 3.9 maximum_convert_fusion
  (119 shorter events, 28.3 us)
Async XLA Ops:
  7.2 22.4 %copy-start.13 = (bf16[1024,384]{1,0:T(8,128)(2,1)S(1)}, bf16[1024,384]{1,0:T(8,128)(2,1)}, u32[]{:S(2)}) copy-start(bf16[1024,384]{1,0:T(8,128)(2,1)} %param.20) | copy-start | bytes 2359300
  7.2 22.5 %copy-start.21 = (bf16[1024,384]{1,0:T(8,128)(2,1)S(1)}, bf16[1024,384]{1,0:T(8,128)(2,1)}, u32[]{:S(2)}) copy-start(bf16[1024,384]{1,0:T(8,128)(2,1)} %param.22) | copy-start | bytes 2359300
  7.2 230.5 %all-reduce.6.cloned.1.call-start = ((), (), s32[]{:S(2)}) async-start(), calls=%async_computation | async-start | bytes 3145728 | tf_op jit(solution)/shard_map/psum | solution.py:932
  7.3 24.3 %collective-permute-start = (bf16[1024,384]{1,0:T(8,128)(2,1)}, bf16[1024,384]{1,0:T(8,128)(2,1)}, u32[]{:S(2)}, u32[]{:S(2)}) collective-permute-start(bf16[1024,384]{1,0:T(8,128)(2,1)} %param.20), channel_id=1, source_target_pairs={{0,1},{1,0},{2,3},{3,2},{4,5},{5,4},{6,7},{7,6},{8,9},{9,8},{10,11... | collective-permute-start | bytes 2359304 | tf_op jit(solution)/shard_map/ppermute | solution.py:304
  7.8 21.0 %collective-permute-start.1 = (bf16[1024,384]{1,0:T(8,128)(2,1)}, bf16[1024,384]{1,0:T(8,128)(2,1)}, u32[]{:S(2)}, u32[]{:S(2)}) collective-permute-start(bf16[1024,384]{1,0:T(8,128)(2,1)} %param.20), channel_id=1, source_target_pairs={{0,2},{2,0},{1,3},{3,1},{4,6},{6,4},{5,7},{7,5},{8,10},{10,8},{9,1... | collective-permute-start | bytes 2359304 | tf_op jit(solution)/shard_map/ppermute | solution.py:300
  28.8 5.3 collective-permute-start.2
  28.8 39.8 %collective-permute-start.4 = (bf16[1024,384]{1,0:T(8,128)(2,1)}, bf16[1024,384]{1,0:T(8,128)(2,1)S(1)}, u32[]{:S(2)}, u32[]{:S(2)}) collective-permute-start(bf16[1024,384]{1,0:T(8,128)(2,1)} %param.22), channel_id=1, source_target_pairs={{0,1},{1,0},{2,3},{3,2},{4,5},{5,4},{6,7},{7,6},{8,9},{9,8},{10,11... | collective-permute-start | bytes 2359304 | tf_op jit(solution)/shard_map/ppermute | solution.py:304
  29.7 38.4 %collective-permute-start.3 = (bf16[1024,384]{1,0:T(8,128)(2,1)S(1)}, bf16[1024,384]{1,0:T(8,128)(2,1)S(1)}, u32[]{:S(2)}, u32[]{:S(2)}) collective-permute-start(bf16[1024,384]{1,0:T(8,128)(2,1)S(1)} %copy-done.21), channel_id=1, source_target_pairs={{0,2},{2,0},{1,3},{3,1},{4,6},{6,4},{5,7},{7,5},{8,10},{10,8},{9,1... | collective-permute-start | bytes 2359304 | tf_op jit(solution)/shard_map/ppermute | solution.py:300
  38.0 3.1 copy-start.8
  38.0 3.1 copy-start.26
  68.2 2.5 collective-permute-start.5
  68.8 5.0 copy-start.1
  68.9 5.0 copy-start.2
  71.9 60.1 %copy-start.9 = (bf16[1024,1536]{1,0:T(8,128)(2,1)}, bf16[1024,1536]{1,0:T(8,128)(2,1)S(1)}, u32[]{:S(2)}) copy-start(bf16[1024,1536]{1,0:T(8,128)(2,1)S(1)} %constant_dynamic-update-slice_fusion) | copy-start | bytes 9437188
  73.8 40.3 %copy-start.24 = (bf16[1536,1152]{1,0:T(8,128)(2,1)S(1)}, bf16[1536,1152]{1,0:T(8,128)(2,1)}, u32[]{:S(2)}) copy-start(bf16[1536,1152]{1,0:T(8,128)(2,1)} %gate_w.1) | copy-start | bytes 10616836
  114.0 4.3 copy-start.3
  114.0 28.2 %copy-start = (f32[256,1536]{1,0:T(8,128)}, f32[256,1536]{1,0:T(8,128)S(1)}, u32[]{:S(2)}) copy-start(f32[256,1536]{1,0:T(8,128)S(1)} %get-tuple-element.79.resid_ref.refs_10_) | copy-start | bytes 4718596
  114.1 4.2 copy-start.25
  118.3 4.2 copy-start.12
  142.2 400.3 %all-reduce.8.cloned.1.call-start = ((), (), s32[]{:S(2)}) async-start(), calls=%async_computation.1 | async-start | bytes 3932160 | tf_op jit(solution)/shard_map/psum | solution.py:944
  237.7 6.4 %copy-start.7 = (bf16[1024,1536]{1,0:T(8,128)(2,1)S(1)}, bf16[1024,1536]{1,0:T(8,128)(2,1)}, u32[]{:S(2)}) copy-start(bf16[1024,1536]{1,0:T(8,128)(2,1)} %copy-done.6) | copy-start | bytes 9437188
  252.7 1.3 collective-permute-start.6
  254.0 3.7 collective-permute-start.7
  538.8 8.4 %copy-start.11 = (bf16[1536,1152]{1,0:T(8,128)(2,1)S(1)}, bf16[1536,1152]{1,0:T(8,128)(2,1)}, u32[]{:S(2)}) copy-start(bf16[1536,1152]{1,0:T(8,128)(2,1)} %get-tuple-element.107) | copy-start | bytes 10616836
  547.1 3.5 copy-start.10
  550.6 3.4 copy-start.19
  554.1 2.1 copy-start.18
  556.2 2.1 copy-start.17
  558.3 3.5 copy-start.23
  558.3 5.3 copy-start.15
  558.3 5.3 copy-start.20
  563.6 4.0 copy-start.22
  (5 other events, 8.2 us)
Sparse Core Ops, SparseCore 0:
  142.3 89.6 all-reduce.5
  244.3 134.2 all-reduce.7

commit v3 on v2

--- a/solution.py
+++ b/solution.py
@@ -920,7 +920,7 @@
     hidden_up = dot(two_low, ffn_up, 1, 0)
     hidden_act, hidden_slope = gelu_parts(hidden_gate)
     hidden_low = (hidden_act * hidden_up).astype(BF16)
-    cut = hidden_low.shape[1] * 4 // 9
+    cut = hidden_low.shape[1] * 5 // 9
     down_early = dot(hidden_low[:, :cut], whole_cot, 0, 0)
     down_late = dot(hidden_low[:, cut:], whole_cot, 0, 0)
     d_hgate = (d_hidden * hidden_up * hidden_slope).astype(BF16)
@@ -939,15 +939,15 @@
     d_gate_low, d_branch_low, misc = backward_block(
         d_mixed, gate_pre, branch_pre, conv, rate, opened, state, masks, rows, rate_weight, input_weight
     )
-    if n_dp == 8:
-        down_early, down_late, d_gate_low = lax.optimization_barrier((down_early, down_late, d_gate_low))
-        down_late = lax.psum(down_late, "dp")
     first_share = dot(d_gate_low, gate_weight, 1, 1) + dot(d_branch_low, branch_weight, 1, 1)
     product = first_share * in_f
     sums = jnp.concatenate([
         jnp.sum(product * q_one, axis=0), second_gain_grad, jnp.sum(product * gain_one, axis=1)
     ])
     sums = tensor_sum(sums.reshape(-1, LANES)).reshape(-1)
+    if n_dp == 8:
+        down_early, down_late, sums = lax.optimization_barrier((down_early, down_late, sums))
+        down_late = lax.psum(down_late, "dp")
     gains = sums[: 2 * features].reshape(-1, channels)
     mean_one = sums[2 * features :, None] / features
     misc = lax.dynamic_update_slice_in_dim(misc, gains.astype(BF16), 2 * LANES + 16, 0)

time: 585 us -> 576 us (0.985)
  no operation moved by 1% of the time
where the time goes in v3:
time: 576 us; the launch traced here: 571 us
  Pallas kernels  429 us (74%)
  matrix products  50.3 us (9%)
  other arithmetic  31.3 us (5%)
  local copies, waits for them, and re-layouts  22.8 us (4%)
  waiting for transfers between devices  16.7 us (3%)
  between operations  15.1 us (3%)
  starting transfers between devices  6.32 us (1%)
    pallas_call x1, Pallas kernels, ring_all(): pl.pallas_call(functools.partial(ring_kernel, given, n), in_specs=[hbm] *...  279 us
    pallas_call x1, Pallas kernels, pull(): pl.pallas_call(pull_kernel, in_specs=[vmem] * 8, out_specs=[pl.BlockSpec(...  50.5 us
    dot_general x10, matrix products, dot(): lax.dot_general(a, b, (((left,), (right,)), ((), ())), preferred_element_...  50.3 us
    pallas_call x1, Pallas kernels, project(): pl.pallas_call(project_kernel, in_specs=[pl.BlockSpec(memory_space=pltpu....  40.2 us
    pallas_call x1, Pallas kernels, backward_block(): pl.pallas_call(backward_kernel, grid=(heads,), in_specs=[col] * 7 + [whol...  34.3 us
    pallas_call x1, Pallas kernels, forward_block(): pl.pallas_call(forward_kernel, grid=(heads,), in_specs=[col, col, whole,...  24.5 us
    convert_element_type x7, other arithmetic, body(): a.astype(F32)  18.2 us
    ppermute x3, waiting for transfers between devices, swap_x(): return lax.ppermute(v, 'tensor', X_PAIRS)  14.2 us
  transfers between devices with their start and end apart: 10, of which 4 were waited for; matrix products, arithmetic and copies ran while one was open for 7% of the time, Pallas kernels for 68%

profile of v3, /device:TPU:0, one launch (start us, length us, event | category | flops | bytes accessed | tf_op | source)
XLA Modules:
  0.0 571.2 jit_solution(16447403303426896916)
XLA Ops:
  7.8 2.6 collective-permute-start.1
  18.0 10.8 %collective-permute-done.1 = bf16[1024,384]{1,0:T(8,128)(2,1)} collective-permute-done((bf16[1024,384]{1,0:T(8,128)(2,1)}, bf16[1024,384]{1,0:T(8,128)(2,1)}, u32[]{:S(2)}, u32[]{:S(2)}) %collective-permute-start.1) | collective-permute-done | bytes 786464 | tf_op jit(solution)/shard_map/ppermute | solution.py:300
  29.7 1.8 collective-permute-start.3
  38.0 3.1 broadcast_add_fusion.branch_ref
  41.1 3.2 broadcast_add_fusion.1.gate_ref
  44.3 24.5 %recurrence_forward.1 = (f32[1024,512]{1,0:T(8,128)}, f32[1024,512]{1,0:T(8,128)}, f32[1024,512]{1,0:T(8,128)}, f32[1024,512]{1,0:T(8,128)}, bf16[1024,512]{1,0:T(8,128)(2,1)}) custom-call(f32[1024,512]{1,0:T(8,128)} %broadcast_add_fusion.1.gate_ref, f32[1024,512]{1,0:T(8,128)} %broadcast_add_fusion.branch_ref, f32[1032,4]{1,0:T(8,128)} %pad_convert_fusion.mask_ref, ...), custom_call_target="tpu_custom_call" | custom-call | flops 367001600 | bytes 13631488 | tf_op jit(solution)/shard_map/recurrence_forward/pallas_call | solution.py:122
  69.6 1.6 collective-permute-done.5
  72.5 1.8 constant_dynamic-slice_fusion
  74.4 40.2 %project.1 = (bf16[1024,1536]{1,0:T(8,128)(2,1)S(1)}, f32[256,1536]{1,0:T(8,128)S(1)}) custom-call(bf16[1024,512]{1,0:T(8,128)(2,1)S(1)} %copy-done.1, bf16[512,1536]{1,0:T(8,128)(2,1)S(1)} %copy-done.2, bf16[256,1536]{1,0:T(8,128)(2,1)S(1)} %get-tuple-element.131.own_ref, f32[1,1536]{1,0:T(1,128)S(1)} %broadcast_in_dim.5.gain_ref), custom_call_target="tpu_custom_call" | custom-call | flops 1610612736 | bytes 125829120 | tf_op jit(solution)/shard_map/project/pallas_call | solution.py:765
  114.6 5.8 %fusion.19 = f32[1024,1152]{1,0:T(8,128)} fusion(bf16[1024,1536]{1,0:T(8,128)(2,1)S(1)} %get-tuple-element.75.two_ref, bf16[1536,1152]{1,0:T(8,128)(2,1)S(1)} %copy-done.27), kind=kOutput, calls=%fused_computation.67 | convolution fusion | flops 3623878656 | bytes 11403264 | tf_op jit(solution)/shard_map/dot_general | solution.py:847
  120.5 5.8 %fusion.20 = f32[1024,1152]{1,0:T(8,128)} fusion(bf16[1024,1536]{1,0:T(8,128)(2,1)S(1)} %get-tuple-element.75.two_ref, bf16[1536,1152]{1,0:T(8,128)(2,1)S(1)} %copy-done.28), kind=kOutput, calls=%fused_computation.68 | convolution fusion | flops 3623878656 | bytes 11403264 | tf_op jit(solution)/shard_map/dot_general | solution.py:847
  126.3 11.0 %multiply_convert_fusion = (bf16[1024,1152]{1,0:T(8,128)(2,1)}, bf16[1024,1152]{1,0:T(8,128)(2,1)}, bf16[1024,1152]{1,0:T(8,128)(2,1)S(1)}) fusion(f32[1024,1152]{1,0:T(8,128)} %fusion.19, f32[1024,1152]{1,0:T(8,128)} %fusion.20, bf16[1024,1536]{1,0:T(8,128)(2,1)S(1)} %constant_dynamic-update-slice_fusion, bf16[1152,1536]{1,0:T(8,128)(2,1)S(1)} %copy-done.14), kind=kOutput, calls=%fused_computation.17 | convolution fusion | flops 3653369856 | bytes 23199744 | tf_op jit(solution)/shard_map/dot_general | solution.py:847
  137.3 1.4 copy-done.16
  138.6 3.0 convolution_convert_fusion.1
  141.7 5.8 %convolution_convert_fusion = bf16[640,1536]{1,0:T(8,128)(2,1)} fusion(bf16[1024,1536]{1,0:T(8,128)(2,1)} %copy-done.10, bf16[1024,1152]{1,0:T(8,128)(2,1)} %copy-done.16), kind=kOutput, calls=%fused_computation.22 | convolution fusion | flops 2014248960 | bytes 6422528 | tf_op jit(solution)/shard_map/dot_general | solution.py:847
  147.5 1.7 copy-done.5
  149.2 1.7 copy-done.6
  150.9 50.5 %pull.1 = (bf16[1024,1536]{1,0:T(8,128)(2,1)}, f32[1,1536]{1,0:T(1,128)S(1)}, bf16[1536,1152]{1,0:T(8,128)(2,1)}, bf16[1536,1152]{1,0:T(8,128)(2,1)}) custom-call(bf16[1024,1152]{1,0:T(8,128)(2,1)S(1)} %copy-done.6, bf16[1024,1152]{1,0:T(8,128)(2,1)S(1)} %copy-done.5, bf16[1536,1152]{1,0:T(8,128)(2,1)} %gate_w.1, bf16[1536,1152]{1,0:T(8,128)(2,1)} %up_w.1, ...), custom_call_target="tpu_custom_call" | custom-call | flops 14495514624 | bytes 125829120 | tf_op jit(solution)/shard_map/pull/pallas_call | solution.py:825
  201.4 5.1 fusion.21.dmix_ref
  206.6 34.3 %recurrence_backward.1 = (bf16[1024,512]{1,0:T(8,128)(2,1)}, bf16[1024,512]{1,0:T(8,128)(2,1)}, bf16[384,512]{1,0:T(8,128)(2,1)}) custom-call(f32[1024,512]{1,0:T(8,128)} %fusion.21.dmix_ref, f32[1024,512]{1,0:T(8,128)} %broadcast_add_fusion.1.gate_ref, f32[1024,512]{1,0:T(8,128)} %broadcast_add_fusion.branch_ref, f32[1024,512]{1,0:T(8,128)} %get-tuple-element.83.conv_ref, ...), custom_call_target="tpu_custom_call" | custom-call | flops 734003200 | bytes 16777216 | tf_op jit(solution)/shard_map/recurrence_backward/pallas_call | solution.py:269
  240.9 3.2 fusion.22
  244.1 4.4 multiply_reduce_fusion.1
  250.1 3.4 collective-permute-done.7
  255.0 279.2 %ring_all.1 = (bf16[1536,1152]{1,0:T(8,128)(2,1)}, bf16[1536,1152]{1,0:T(8,128)(2,1)}, bf16[384,512]{1,0:T(8,128)(2,1)}, bf16[1536,512]{1,0:T(8,128)(2,1)}, bf16...) custom-call(bf16[1536,1152]{1,0:T(8,128)(2,1)} %get-tuple-element.80.refs_0_, ...), custom_call_target="tpu_custom_call" | custom-call | flops 12189696 | bytes 609484800 | tf_op jit(solution)/shard_map/ring_all/pallas_call | solution.py:597
  534.2 3.7 multiply_subtract_fusion
  539.8 1.4 fusion.18
  542.5 3.5 convert_element_type.98
  546.0 3.4 convert_element_type.99
  549.5 2.1 convert_element_type.95
  551.6 2.1 convert_element_type.96
  553.7 2.1 convert_element_type.97
  559.0 3.9 maximum_convert_fusion
  (127 shorter events, 28.1 us)
Async XLA Ops:
  7.2 22.4 %copy-start.15 = (bf16[1024,384]{1,0:T(8,128)(2,1)S(1)}, bf16[1024,384]{1,0:T(8,128)(2,1)}, u32[]{:S(2)}) copy-start(bf16[1024,384]{1,0:T(8,128)(2,1)} %param.20) | copy-start | bytes 2359300
  7.2 22.5 %copy-start.24 = (bf16[1024,384]{1,0:T(8,128)(2,1)S(1)}, bf16[1024,384]{1,0:T(8,128)(2,1)}, u32[]{:S(2)}) copy-start(bf16[1024,384]{1,0:T(8,128)(2,1)} %param.22) | copy-start | bytes 2359300
  7.2 246.3 %all-reduce.6.cloned.1.call-start = ((), (), s32[]{:S(2)}) async-start(), calls=%async_computation | async-start | bytes 3932160 | tf_op jit(solution)/shard_map/psum | solution.py:932
  7.3 24.3 %collective-permute-start = (bf16[1024,384]{1,0:T(8,128)(2,1)}, bf16[1024,384]{1,0:T(8,128)(2,1)}, u32[]{:S(2)}, u32[]{:S(2)}) collective-permute-start(bf16[1024,384]{1,0:T(8,128)(2,1)} %param.20), channel_id=1, source_target_pairs={{0,1},{1,0},{2,3},{3,2},{4,5},{5,4},{6,7},{7,6},{8,9},{9,8},{10,11... | collective-permute-start | bytes 2359304 | tf_op jit(solution)/shard_map/ppermute | solution.py:304
  7.8 21.0 %collective-permute-start.1 = (bf16[1024,384]{1,0:T(8,128)(2,1)}, bf16[1024,384]{1,0:T(8,128)(2,1)}, u32[]{:S(2)}, u32[]{:S(2)}) collective-permute-start(bf16[1024,384]{1,0:T(8,128)(2,1)} %param.20), channel_id=1, source_target_pairs={{0,2},{2,0},{1,3},{3,1},{4,6},{6,4},{5,7},{7,5},{8,10},{10,8},{9,1... | collective-permute-start | bytes 2359304 | tf_op jit(solution)/shard_map/ppermute | solution.py:300
  28.8 5.3 collective-permute-start.2
  28.8 40.4 %collective-permute-start.4 = (bf16[1024,384]{1,0:T(8,128)(2,1)}, bf16[1024,384]{1,0:T(8,128)(2,1)S(1)}, u32[]{:S(2)}, u32[]{:S(2)}) collective-permute-start(bf16[1024,384]{1,0:T(8,128)(2,1)} %param.22), channel_id=1, source_target_pairs={{0,1},{1,0},{2,3},{3,2},{4,5},{5,4},{6,7},{7,6},{8,9},{9,8},{10,11... | collective-permute-start | bytes 2359304 | tf_op jit(solution)/shard_map/ppermute | solution.py:304
  29.7 39.0 %collective-permute-start.3 = (bf16[1024,384]{1,0:T(8,128)(2,1)S(1)}, bf16[1024,384]{1,0:T(8,128)(2,1)S(1)}, u32[]{:S(2)}, u32[]{:S(2)}) collective-permute-start(bf16[1024,384]{1,0:T(8,128)(2,1)S(1)} %copy-done.24), channel_id=1, source_target_pairs={{0,2},{2,0},{1,3},{3,1},{4,6},{6,4},{5,7},{7,5},{8,10},{10,8},{9,1... | collective-permute-start | bytes 2359304 | tf_op jit(solution)/shard_map/ppermute | solution.py:300
  68.7 2.5 collective-permute-start.5
  69.4 5.0 copy-start.1
  69.4 5.0 copy-start.2
  72.5 64.7 %copy-start.10 = (bf16[1024,1536]{1,0:T(8,128)(2,1)}, bf16[1024,1536]{1,0:T(8,128)(2,1)S(1)}, u32[]{:S(2)}) copy-start(bf16[1024,1536]{1,0:T(8,128)(2,1)S(1)} %constant_dynamic-update-slice_fusion) | copy-start | bytes 9437188
  74.4 40.3 %copy-start.27 = (bf16[1536,1152]{1,0:T(8,128)(2,1)S(1)}, bf16[1536,1152]{1,0:T(8,128)(2,1)}, u32[]{:S(2)}) copy-start(bf16[1536,1152]{1,0:T(8,128)(2,1)} %gate_w.1) | copy-start | bytes 10616836
  114.6 5.9 %copy-start.4 = (bf16[1024,1536]{1,0:T(8,128)(2,1)}, bf16[1024,1536]{1,0:T(8,128)(2,1)S(1)}, u32[]{:S(2)}) copy-start(bf16[1024,1536]{1,0:T(8,128)(2,1)S(1)} %get-tuple-element.75.two_ref) | copy-start | bytes 9437188
  114.6 32.9 %copy-start = (f32[256,1536]{1,0:T(8,128)}, f32[256,1536]{1,0:T(8,128)S(1)}, u32[]{:S(2)}) copy-start(f32[256,1536]{1,0:T(8,128)S(1)} %get-tuple-element.79.resid_ref.refs_10_) | copy-start | bytes 4718596
  114.6 5.8 %copy-start.28 = (bf16[1536,1152]{1,0:T(8,128)(2,1)S(1)}, bf16[1536,1152]{1,0:T(8,128)(2,1)}, u32[]{:S(2)}) copy-start(bf16[1536,1152]{1,0:T(8,128)(2,1)} %up_w.1) | copy-start | bytes 10616836
  120.5 5.8 %copy-start.14 = (bf16[1152,1536]{1,0:T(8,128)(2,1)S(1)}, bf16[1152,1536]{1,0:T(8,128)(2,1)}, u32[]{:S(2)}) copy-start(bf16[1152,1536]{1,0:T(8,128)(2,1)} %refs_9_.1) | copy-start | bytes 10616836
  147.5 390.4 %all-reduce.8.cloned.1.call-start = ((), (), s32[]{:S(2)}) async-start(), calls=%async_computation.1 | async-start | bytes 3145728 | tf_op jit(solution)/shard_map/psum | solution.py:950
  150.9 50.6 %copy-start.3 = (bf16[512,1536]{1,0:T(8,128)(2,1)S(1)}, bf16[512,1536]{1,0:T(8,128)(2,1)}, u32[]{:S(2)}) copy-start(bf16[512,1536]{1,0:T(8,128)(2,1)} %weight_ref.1) | copy-start | bytes 4718596
  206.6 34.3 %copy-start.30 = (bf16[1536,512]{1,0:T(8,128)(2,1)S(1)}, bf16[1536,512]{1,0:T(8,128)(2,1)}, u32[]{:S(2)}) copy-start(bf16[1536,512]{1,0:T(8,128)(2,1)} %param.24) | copy-start | bytes 4718596
  240.8 3.2 copy-start.8
  240.9 3.2 copy-start.11
  240.9 3.2 copy-start.19
  248.5 1.2 collective-permute-start.6
  249.7 3.7 collective-permute-start.7
  534.1 8.4 %copy-start.13 = (bf16[1536,1152]{1,0:T(8,128)(2,1)S(1)}, bf16[1536,1152]{1,0:T(8,128)(2,1)}, u32[]{:S(2)}) copy-start(bf16[1536,1152]{1,0:T(8,128)(2,1)} %get-tuple-element.107) | copy-start | bytes 10616836
  542.5 3.5 copy-start.12
  546.0 3.4 copy-start.22
  553.7 3.5 copy-start.26
  553.7 5.3 copy-start.17
  553.7 5.3 copy-start.23
  559.0 4.0 copy-start.25
  (9 other events, 18.6 us)
Sparse Core Ops, SparseCore 0:
  147.6 98.7 all-reduce.5
  253.6 124.9 all-reduce.7
